TPU v7x, 128 devices: a whole 4x4x4 slice. The times are simulated.
128 devices in a mesh: seq: 16 (over y, x), dp: 8 (over z, core).
Axes of the slice: x: 4, y: 4, z: 4, core: 2. Of those that a mesh axis runs over, the one named last changes fastest.
Arguments:
- points: bfloat16 [8, 16384, 256], P('dp', 'seq'), may hold values from -6 to 6
- targets: int32 [8, 16384], P('dp', 'seq'), may hold values from 0 to 16383, as said below
- cotangent: bfloat16 [8, 16384, 256], P('dp', 'seq'), may hold values from -6 to 6
- w_qkv: bfloat16 [256, 768], replicated
- w_out: bfloat16 [256, 256], replicated, may hold values from -0.375 to 0.375
- w_up: bfloat16 [256, 1024], replicated, may hold values from -0.375 to 0.375
- w_down: bfloat16 [1024, 256], replicated, may hold values from -0.1875 to 0.1875
Outputs:
- result: bfloat16 [8, 16384, 256], P('dp', 'seq')
- grad_points: bfloat16 [8, 16384, 256], P('dp', 'seq')
- grad_qkv: float32 [256, 768], replicated
- grad_out: float32 [256, 256], replicated
- grad_up: float32 [256, 1024], replicated
- grad_down: float32 [1024, 256], replicated
Inputs may be any that keep to these rules, and one draw needn't show every extreme that they name: In each tile, targets is a permutation of the tile's positions. With owner = target // 1024, the points held by one index of seq send at most 128 points to any one owner, and exactly 128 to one owner.
All inputs are finite; a program needn't handle non-finite values.
Results may differ from a plain program's by a relative error of at most 0.035.
The roundings to bfloat16 on the way count: a program that leaves them out, or rounds other values in their place, can miss the bound.
Values may be sent and summed in bfloat16 or wider, within the bound.
A program may use at most 64 MiB of HBM per device.

v0:
```python
import math

import jax
import jax.numpy as jnp
from jax import lax
from jax.sharding import PartitionSpec as P

HEADS = 16
PATCH = 1024


EPS = 1e-05
GELU_A = 0.7978845608028654
GELU_B = 0.044715


def normalize(values):
    center = jnp.mean(values, axis=-1, keepdims=True)
    shifted = values - center
    inverse_std = lax.rsqrt(jnp.mean(shifted * shifted, axis=-1, keepdims=True) + EPS)
    return (shifted * inverse_std, inverse_std)


def norm_back(normed, inverse_std, upstream):
    return inverse_std * (
        upstream
        - jnp.mean(upstream, axis=-1, keepdims=True)
        - normed * jnp.mean(upstream * normed, axis=-1, keepdims=True)
    )


def gelu_pair(inputs):
    tangent = jnp.tanh(GELU_A * (inputs + GELU_B * inputs * inputs * inputs))
    outputs = 0.5 * inputs * (1.0 + tangent)
    slopes = 0.5 * (1.0 + tangent) + 0.5 * inputs * (1.0 - tangent * tangent) * GELU_A * (
        1.0 + 3.0 * GELU_B * inputs * inputs
    )
    return (outputs, slopes)


def contract_rows(left, right):
    return lax.dot_general(
        left, right, (((0,), (0,)), ((), ())), preferred_element_type=jnp.float32
    )


def contract_last(left, right):
    return lax.dot_general(
        left, right, (((1,), (1,)), ((), ())), preferred_element_type=jnp.float32
    )


def split_heads(packed, heads):
    row_count = packed.shape[0]
    head_size = packed.shape[1] // (3 * heads)
    shaped = packed.reshape(row_count // PATCH, PATCH, 3, heads, head_size)
    return shaped.transpose(2, 0, 3, 1, 4).reshape(3, row_count // PATCH * heads, PATCH, head_size)


def split_single(packed, heads):
    row_count = packed.shape[0]
    head_size = packed.shape[1] // heads
    shaped = packed.reshape(row_count // PATCH, PATCH, heads, head_size)
    return shaped.transpose(0, 2, 1, 3).reshape(row_count // PATCH * heads, PATCH, head_size)


def merge_heads(stacked, row_count, heads):
    head_size = stacked.shape[-1]
    shaped = stacked.reshape(row_count // PATCH, heads, PATCH, head_size)
    return shaped.transpose(0, 2, 1, 3).reshape(row_count, heads * head_size)


def merge_triple(stacked, row_count, heads):
    head_size = stacked.shape[-1]
    shaped = stacked.reshape(row_count // PATCH, heads, 3, PATCH, head_size)
    return shaped.transpose(0, 3, 2, 1, 4).reshape(row_count, 3 * heads * head_size)


def head_probs(queries, keys_head):
    factor = queries.shape[-1] ** (-0.5)
    scores = contract_last(queries, keys_head) * factor
    scores = scores - jnp.max(scores, axis=-1, keepdims=True)
    raised = jnp.exp(scores)
    return raised / jnp.sum(raised, axis=-1, keepdims=True)


def head_forward(members):
    queries, keys_head, values_head = members
    weights_soft = head_probs(queries, keys_head).astype(jnp.bfloat16)
    return jnp.dot(weights_soft, values_head, preferred_element_type=jnp.float32).astype(
        jnp.bfloat16
    )


def head_backward(members):
    queries, keys_head, values_head, outputs, upstream = members
    factor = queries.shape[-1] ** (-0.5)
    weights_soft = head_probs(queries, keys_head)
    rounded = weights_soft.astype(jnp.bfloat16)
    grad_values = contract_rows(rounded, upstream)
    grad_weights = contract_last(upstream, values_head)
    row_inner = jnp.sum(
        upstream.astype(jnp.float32) * outputs.astype(jnp.float32), axis=-1, keepdims=True
    )
    grad_scores = (weights_soft * (grad_weights - row_inner)).astype(jnp.bfloat16)
    grad_queries = jnp.dot(grad_scores, keys_head, preferred_element_type=jnp.float32) * factor
    grad_keys = contract_rows(grad_scores, queries) * factor
    return jnp.stack([grad_queries, grad_keys, grad_values]).astype(jnp.bfloat16)


def attend(packed, heads):
    pieces = split_heads(packed, heads)
    outputs = lax.map(head_forward, (pieces[0], pieces[1], pieces[2]))
    return merge_heads(outputs, packed.shape[0], heads)


def attend_back(packed, attended, upstream, heads):
    pieces = split_heads(packed, heads)
    out_items = split_single(attended, heads)
    grad_items = split_single(upstream, heads)
    gradients = lax.map(head_backward, (pieces[0], pieces[1], pieces[2], out_items, grad_items))
    return merge_triple(gradients, packed.shape[0], heads)


def pack_rows(values, slot_index, peer_count, slot_room):
    buffer = (
        jnp.zeros((peer_count * slot_room, values.shape[1]), values.dtype)
        .at[slot_index]
        .set(values)
    )
    return buffer.reshape(peer_count, slot_room, values.shape[1])


def place_rows(received, places, row_count):
    flattened = received.reshape(-1, received.shape[2])
    return (
        jnp.zeros((row_count, flattened.shape[1]), flattened.dtype)
        .at[places]
        .set(flattened, mode="drop")
    )


def gather_back(values, places, row_count, peer_count, slot_room):
    is_valid = (places < row_count)[:, None]
    picked = jnp.where(
        is_valid, values[jnp.minimum(places, row_count - 1)], jnp.zeros((), values.dtype)
    )
    return picked.reshape(peer_count, slot_room, values.shape[1])


def unpack_rows(received, slot_index):
    return received.reshape(-1, received.shape[2])[slot_index]


def feed_forward(features, restored, tile_grad, w_out, w_up, w_down):
    hidden = features + jnp.dot(restored, w_out, preferred_element_type=jnp.float32)
    normed_second, inverse_second = normalize(hidden)
    second_rows = normed_second.astype(jnp.bfloat16)
    expanded = jnp.dot(second_rows, w_up, preferred_element_type=jnp.float32)
    activated, slopes = gelu_pair(expanded)
    activated = activated.astype(jnp.bfloat16)
    result = (hidden + jnp.dot(activated, w_down, preferred_element_type=jnp.float32)).astype(
        jnp.bfloat16
    )
    grad_active = contract_last(tile_grad, w_down)
    grad_expand = (grad_active * slopes).astype(jnp.bfloat16)
    grad_second = contract_last(grad_expand, w_up)
    grad_hidden = tile_grad.astype(jnp.float32) + norm_back(
        normed_second, inverse_second, grad_second
    )
    hidden_rows = grad_hidden.astype(jnp.bfloat16)
    weight_out = contract_rows(restored, hidden_rows)
    weight_up = contract_rows(second_rows, grad_expand)
    weight_down = contract_rows(activated, tile_grad)
    return (result, grad_hidden, hidden_rows, weight_out, weight_up, weight_down)


def body(points, targets, cotangent, w_qkv, w_out, w_up, w_down):
    row_count = points.shape[1]
    peer_count = lax.axis_size("seq")
    slot_room = 2 * row_count // peer_count
    destination = targets[0]
    owner = destination // row_count
    local_place = destination - owner * row_count
    marks = (owner[:, None] == jnp.arange(peer_count, dtype=jnp.int32)[None, :]).astype(jnp.int32)
    ranking = jnp.sum((jnp.cumsum(marks, axis=0) - 1) * marks, axis=1)
    slot_index = owner * slot_room + ranking
    place_buffer = (
        jnp.full((peer_count * slot_room,), row_count, jnp.int32)
        .at[slot_index]
        .set(local_place)
        .reshape(peer_count, slot_room)
    )
    features = points[0].astype(jnp.float32)
    tile_grad = cotangent[0]
    normed_first, inverse_first = normalize(features)
    first_rows = normed_first.astype(jnp.bfloat16)
    projected = jnp.dot(first_rows, w_qkv, preferred_element_type=jnp.float32).astype(jnp.bfloat16)
    received, places = (
        lax.all_to_all(
            pack_rows(projected, slot_index, peer_count, slot_room),
            "seq",
            split_axis=0,
            concat_axis=0,
            tiled=True,
        ),
        lax.all_to_all(place_buffer, "seq", split_axis=0, concat_axis=0, tiled=True),
    )
    places = places.reshape(-1)
    ordered = place_rows(received, places, row_count)
    attended = attend(ordered, HEADS)
    returned = lax.all_to_all(
        gather_back(attended, places, row_count, peer_count, slot_room),
        "seq",
        split_axis=0,
        concat_axis=0,
        tiled=True,
    )
    restored = unpack_rows(returned, slot_index)
    result, grad_hidden, hidden_rows, weight_out, weight_up, weight_down = feed_forward(
        features, restored, tile_grad, w_out, w_up, w_down
    )
    grad_attended = contract_last(hidden_rows, w_out).astype(jnp.bfloat16)
    grad_arrived = lax.all_to_all(
        pack_rows(grad_attended, slot_index, peer_count, slot_room),
        "seq",
        split_axis=0,
        concat_axis=0,
        tiled=True,
    )
    grad_ordered = attend_back(
        ordered, attended, place_rows(grad_arrived, places, row_count), HEADS
    )
    grad_returned = lax.all_to_all(
        gather_back(grad_ordered, places, row_count, peer_count, slot_room),
        "seq",
        split_axis=0,
        concat_axis=0,
        tiled=True,
    )
    grad_projected = unpack_rows(grad_returned, slot_index)
    grad_first = contract_last(grad_projected, w_qkv).astype(jnp.bfloat16)
    weight_first = contract_rows(first_rows, grad_projected)
    grad_input = (
        grad_hidden + norm_back(normed_first, inverse_first, grad_first.astype(jnp.float32))
    ).astype(jnp.bfloat16)
    summed = lax.psum((weight_first, weight_out, weight_up, weight_down), ("seq", "dp"))
    factor = 1.0 / math.sqrt(points.shape[0] * lax.axis_size("dp") * peer_count * row_count)
    return (
        result[None],
        grad_input[None],
        summed[0] * factor,
        summed[1] * factor,
        summed[2] * factor,
        summed[3] * factor,
    )


def solution(mesh):
    return jax.shard_map(
        body,
        mesh=mesh,
        in_specs=(P("dp", "seq", None), P("dp", "seq"), P("dp", "seq", None), P(), P(), P(), P()),
        out_specs=(P("dp", "seq", None), P("dp", "seq", None), P(), P(), P(), P()),
        check_vma=False,
    )
```

profile of v0, /device:TPU:1, one launch (start us, length us, event | category | flops | bytes accessed | tf_op | source)
XLA Modules:
  0.0 591.2 jit_solution(18257109326253834183)
XLA Ops:
  8.6 4.5 reduce-window.6
  14.3 4.9 scatter_custom_fusion
  19.2 7.6 %all-to-all-start = ((s32[16,1,128]{2,1,0:T(1,128)}), s32[16,1,128]{2,1,0:T(1,128)S(1)}, u32[]{:S(2)}, u32[]{:S(2)}) async-start(s32[16,1,128]{2,1,0:T(1,128)} %bitcast.20), calls=%async_computation | async-start | bytes 16384 | tf_op jit(solution)/shard_map/all_to_all | solution.py:207
  28.4 2.8 convolution_convert_fusion
  31.2 7.9 %scatter_custom_fusion.1 = bf16[2048,768]{1,0:T(8,128)(2,1)} fusion(s32[1024]{0:T(1024)S(1)} %bitcast.245, bf16[1024,768]{1,0:T(8,128)(2,1)} %convolution_convert_fusion, bf16[]{:T(256)} %constant.96.clone.1), kind=kCustom, calls=%fused_computation.82 | custom fusion | bytes 3146240 | tf_op jit(solution)/shard_map/scatter | solution.py:129
  39.1 6.7 %all-to-all-start.1 = ((bf16[16,128,768]{2,1,0:T(8,128)(2,1)}), bf16[16,128,768]{2,1,0:T(8,128)(2,1)}, u32[]{:S(2)}, u32[]{:S(2)}) async-start(bf16[16,128,768]{2,1,0:T(8,128)(2,1)} %bitcast.229), calls=%async_computation.1 | async-start | bytes 6291456 | tf_op jit(solution)/shard_map/all_to_all | solution.py:200
  45.9 45.1 %all-to-all-done.1 = bf16[16,128,768]{2,1,0:T(8,128)(2,1)} async-done(((bf16[16,128,768]{2,1,0:T(8,128)(2,1)}), bf16[16,128,768]{2,1,0:T(8,128)(2,1)}, u32[]{:S(2)}, u32[]{:S(2)}) %all-to-all-start.1) | async-done | bytes 3145760 | tf_op jit(solution)/shard_map/all_to_all | solution.py:200
  90.9 11.4 %scatter_custom_fusion.2 = bf16[1024,768]{1,0:T(8,128)(2,1)} fusion(s32[2048]{0:T(1024)S(1)} %bitcast.248, bf16[2048,768]{1,0:T(8,128)(2,1)} %bitcast.26, bf16[]{:T(256)} %constant.96.clone.1), kind=kCustom, calls=%fused_computation.109 | custom fusion | bytes 1573376 | tf_op jit(solution)/shard_map/scatter | solution.py:139
  102.3 2.6 copy.67
  106.4 37.9 %while.20 = (s32[]{:T(128)}, bf16[16,1024,16]{1,2,0:T(8,128)(2,1)S(1)}, bf16[16,1024,16]{1,2,0:T(8,128)(2,1)S(1)}, bf16[16,1024,16]{1,2,0:T(8,128)(2,1)S(1)}, bf16[16,1024,16]{1,2,0:T(8,128)(2,1)S(1)}, /*index=5*/s32[]{:T(128)}) while((s32[]{:T(128)}, bf16[16,1024,16]{1,2,0:T(8,128)(2,1)S(1)}, bf16[16,1024,16]{1,2,0:T(8,128)(2,1)S(1)}, ...), condition=%wide.region_11.12_spmd, body=%wide.region_8.11_spmd.sunk | while | flops 76560384 | bytes 12736589 | solution.py:113
  145.7 7.5 %gather_fusion = bf16[2048,256]{1,0:T(8,128)(2,1)S(1)} fusion(bf16[1024,256]{1,0:T(8,128)(2,1)S(1)} %copy.68, s32[2048]{0:T(1024)S(1)} %broadcast_clamp_fusion), kind=kCustom, calls=%fused_computation | custom fusion | bytes 2105344 | tf_op jit(solution)/shard_map/gather | solution.py:146
  154.5 3.8 all-to-all-start.2
  159.5 13.7 %all-to-all-done.2 = bf16[16,128,256]{2,1,0:T(8,128)(2,1)S(1)} async-done(((bf16[16,128,256]{2,1,0:T(8,128)(2,1)}), bf16[16,128,256]{2,1,0:T(8,128)(2,1)S(1)}, u32[]{:S(2)}, u32[]{:S(2)}) %all-to-all-start.2) | async-done | bytes 1048608 | tf_op jit(solution)/shard_map/all_to_all | solution.py:212
  173.2 3.9 gather_fusion.1
  178.8 2.9 fusion.59
  183.9 1.6 convolution_convert_fusion.1
  185.5 6.0 %scatter_custom_fusion.3 = bf16[2048,256]{1,0:T(8,128)(2,1)} fusion(s32[1024]{0:T(1024)S(1)} %bitcast.247, bf16[1024,256]{1,0:T(8,128)(2,1)S(1)} %convolution_convert_fusion.1, bf16[]{:T(256)} %constant.96.clone.1), kind=kCustom, calls=%fused_computation.120 | custom fusion | bytes 1048578 | tf_op jit(solution)/shard_map/scatter | solution.py:129
  191.5 4.0 all-to-all-start.3
  195.6 14.2 %all-to-all-done.3 = bf16[16,128,256]{2,1,0:T(8,128)(2,1)S(1)} async-done(((bf16[16,128,256]{2,1,0:T(8,128)(2,1)}), bf16[16,128,256]{2,1,0:T(8,128)(2,1)S(1)}, u32[]{:S(2)}, u32[]{:S(2)}) %all-to-all-start.3) | async-done | bytes 1048608 | tf_op jit(solution)/shard_map/all_to_all | solution.py:224
  209.8 9.4 %scatter_custom_fusion.4 = bf16[1024,256]{1,0:T(8,128)(2,1)S(1)} fusion(s32[2048]{0:T(1024)S(1)} %bitcast.249, bf16[2048,256]{1,0:T(8,128)(2,1)S(1)} %bitcast.234, bf16[]{:T(256)} %constant.96.clone.1), kind=kCustom, calls=%fused_computation.127 | custom fusion | bytes 524290 | tf_op jit(solution)/shard_map/scatter | solution.py:139
  219.3 136.4 %while.21 = (s32[]{:T(128)}, bf16[16,3,1024,16]{2,3,0,1:T(8,128)(2,1)S(1)}, bf16[16,1024,16]{1,2,0:T(8,128)(2,1)}, bf16[16,1024,16]{1,2,0:T(8,128)(2,1)}, bf16[1...) while((s32[]{:T(128)}, ...), condition=%wide.region_22.23_spmd, body=%wide.region_18.22_spmd.sunk | while | flops 183940096 | bytes 23697520 | solution.py:121
  220.1 1.5 multiply_reduce_fusion.7
  223.3 2.0 multiply_convert_fusion.5
  228.7 1.5 multiply_reduce_fusion.7
  231.8 2.0 multiply_convert_fusion.5
  240.3 2.0 multiply_convert_fusion.5
  245.7 1.5 multiply_reduce_fusion.7
  248.9 2.0 multiply_convert_fusion.5
  254.2 1.5 multiply_reduce_fusion.7
  257.4 2.0 multiply_convert_fusion.5
  262.8 1.5 multiply_reduce_fusion.7
  265.9 2.0 multiply_convert_fusion.5
  271.3 1.5 multiply_reduce_fusion.7
  274.4 2.0 multiply_convert_fusion.5
  279.8 1.5 multiply_reduce_fusion.7
  282.9 2.0 multiply_convert_fusion.5
  288.3 1.5 multiply_reduce_fusion.7
  291.5 2.0 multiply_convert_fusion.5
  296.8 1.5 multiply_reduce_fusion.7
  300.0 2.0 multiply_convert_fusion.5
  305.4 1.5 multiply_reduce_fusion.7
  308.5 2.0 multiply_convert_fusion.5
  317.0 2.0 multiply_convert_fusion.5
  325.6 2.0 multiply_convert_fusion.5
  330.9 1.5 multiply_reduce_fusion.7
  334.1 2.0 multiply_convert_fusion.5
  342.6 2.0 multiply_convert_fusion.5
  351.1 2.0 multiply_convert_fusion.5
  356.4 9.5 %gather_fusion.2 = bf16[2048,768]{1,0:T(8,128)(2,1)} fusion(bf16[1024,768]{1,0:T(8,128)(2,1)S(1)} %copy.73, s32[2048]{0:T(1024)S(1)} %broadcast_clamp_fusion), kind=kCustom, calls=%fused_computation.2 | custom fusion | bytes 6299648 | tf_op jit(solution)/shard_map/gather | solution.py:146
  365.9 3.3 broadcast_select_fusion
  369.2 3.8 all-to-all-start.4
  373.3 2.6 fusion.87
  375.9 3.6 fusion.92
  379.5 2.6 fusion.79
  382.1 27.7 %all-to-all-done.4 = bf16[16,128,768]{2,1,0:T(8,128)(2,1)S(1)} async-done(((bf16[16,128,768]{2,1,0:T(8,128)(2,1)}), bf16[16,128,768]{2,1,0:T(8,128)(2,1)S(1)}, u32[]{:S(2)}, u32[]{:S(2)}) %all-to-all-start.4) | async-done | bytes 3145760 | tf_op jit(solution)/shard_map/all_to_all | solution.py:234
  409.8 5.2 gather_fusion.3
  415.0 3.1 fusion.84
  418.2 4.9 fusion.68
  423.2 2.0 copy.74
  425.9 1.6 fusion.78
  428.5 148.6 %all-reduce.3.cloned.1.call-done = (f32[256,768]{1,0:T(8,128)}, f32[256,256]{1,0:T(8,128)}, f32[256,1024]{1,0:T(8,128)}, f32[1024,256]{1,0:T(8,128)}) async-done(((f32[256,768]{1,0:T(8,128)}, f32[256,256]{1,0:T(8,128)}, f32[256,1024]{1,0:T(8,128)}, f32[1024,256]{1,0:T(8,128)}), (f32[256,768]{1,0:T(8,128)}, f32[256,256]{1,0:T(8,128)}, f32[256,1024]{1,0:T(8,128)}, ...) | async-done | bytes 3145744 | tf_op jit(solution)/shard_map/psum | solution.py:247
  577.1 2.2 broadcast_multiply_fusion.2
  579.3 1.7 broadcast_multiply_fusion.3
  580.9 2.3 broadcast_multiply_fusion.1
  (243 shorter events, 142.1 us)
Async XLA Ops:
  7.2 170.6 %copy-start = (bf16[256,1024]{1,0:T(8,128)(2,1)S(1)}, bf16[256,1024]{1,0:T(8,128)(2,1)}, u32[]{:S(2)}) copy-start(bf16[256,1024]{1,0:T(8,128)(2,1)} %param.16) | copy-start | bytes 1572868
  19.2 19.9 %all-to-all-start = ((s32[16,1,128]{2,1,0:T(1,128)}), s32[16,1,128]{2,1,0:T(1,128)S(1)}, u32[]{:S(2)}, u32[]{:S(2)}) async-start(s32[16,1,128]{2,1,0:T(1,128)} %bitcast.20), calls=%async_computation | async-start | bytes 16384 | tf_op jit(solution)/shard_map/all_to_all | solution.py:207
  28.1 149.1 %copy-start.4 = (bf16[1,1024,256]{1,2,0:T(8,128)(2,1)}, bf16[1,1024,256]{1,2,0:T(8,128)(2,1)S(1)}, u32[]{:S(2)}) copy-start(bf16[1,1024,256]{1,2,0:T(8,128)(2,1)S(1)} %copy.63) | copy-start | bytes 1572868
  28.2 10.9 %copy-start.20 = (f32[1024]{0:T(1024)}, f32[1024]{0:T(1024)S(1)}, u32[]{:S(2)}) copy-start(f32[1024]{0:T(1024)S(1)} %broadcast_multiply_fusion.9) | copy-start | bytes 12292
  28.4 10.7 %copy-start.22 = (f32[1024]{0:T(1024)}, f32[1024]{0:T(1024)S(1)}, u32[]{:S(2)}) copy-start(f32[1024]{0:T(1024)S(1)} %add_rsqrt_fusion.1) | copy-start | bytes 12292
  39.1 51.8 %all-to-all-start.1 = ((bf16[16,128,768]{2,1,0:T(8,128)(2,1)}), bf16[16,128,768]{2,1,0:T(8,128)(2,1)}, u32[]{:S(2)}, u32[]{:S(2)}) async-start(bf16[16,128,768]{2,1,0:T(8,128)(2,1)} %bitcast.229), calls=%async_computation.1 | async-start | bytes 6291456 | tf_op jit(solution)/shard_map/all_to_all | solution.py:200
  144.4 0.8 copy-start.10
  144.4 1.0 copy-start.14
  144.4 1.1 copy-start.17
  144.4 8.8 %copy-start.11 = (bf16[16,1024,16]{1,2,0:T(8,128)(2,1)}, bf16[16,1024,16]{1,2,0:T(8,128)(2,1)S(1)}, u32[]{:S(2)}) copy-start(bf16[16,1024,16]{1,2,0:T(8,128)(2,1)S(1)} %get-tuple-element.292) | copy-start | bytes 1572868
  154.5 22.7 %copy-start.18 = (bf16[256,256]{1,0:T(8,128)(2,1)S(1)}, bf16[256,256]{1,0:T(8,128)(2,1)}, u32[]{:S(2)}) copy-start(bf16[256,256]{1,0:T(8,128)(2,1)} %param.15) | copy-start | bytes 393220
  154.5 18.7 %all-to-all-start.2 = ((bf16[16,128,256]{2,1,0:T(8,128)(2,1)}), bf16[16,128,256]{2,1,0:T(8,128)(2,1)S(1)}, u32[]{:S(2)}, u32[]{:S(2)}) async-start(bf16[16,128,256]{2,1,0:T(8,128)(2,1)} %broadcast_select_fusion.1), calls=%async_computation.2 | async-start | bytes 2097152 | tf_op jit(solution)/shard_map/all_to_all | solution.py:212
  177.2 1.3 copy-start.6
  177.2 1.3 copy-start.15
  177.2 1.6 copy-start.24
  177.6 5.1 copy-start.2
  178.8 2.9 copy-start.7
  181.8 2.1 copy-start.9
  191.5 18.2 %all-to-all-start.3 = ((bf16[16,128,256]{2,1,0:T(8,128)(2,1)}), bf16[16,128,256]{2,1,0:T(8,128)(2,1)S(1)}, u32[]{:S(2)}, u32[]{:S(2)}) async-start(bf16[16,128,256]{2,1,0:T(8,128)(2,1)} %bitcast.41), calls=%async_computation.3 | async-start | bytes 2097152 | tf_op jit(solution)/shard_map/all_to_all | solution.py:224
  369.2 40.6 %all-to-all-start.4 = ((bf16[16,128,768]{2,1,0:T(8,128)(2,1)}), bf16[16,128,768]{2,1,0:T(8,128)(2,1)S(1)}, u32[]{:S(2)}, u32[]{:S(2)}) async-start(bf16[16,128,768]{2,1,0:T(8,128)(2,1)} %broadcast_select_fusion), calls=%async_computation.4 | async-start | bytes 6291456 | tf_op jit(solution)/shard_map/all_to_all | solution.py:234
  373.0 204.1 %all-reduce.3.cloned.1.call-start = ((), (), s32[]{:S(2)}) async-start(), calls=%async_computation.5 | async-start | bytes 6291456 | tf_op jit(solution)/shard_map/psum | solution.py:247
  373.3 6.2 %copy-start.8 = (f32[1024,1024]{1,0:T(8,128)S(1)}, f32[1024,1024]{1,0:T(8,128)}, u32[]{:S(2)}) copy-start(f32[1024,1024]{1,0:T(8,128)} %copy-done.7) | copy-start | bytes 12582916
  373.3 6.2 %copy-start.16 = (bf16[1,1024,256]{2,1,0:T(8,128)(2,1)S(1)}, bf16[1,1024,256]{2,1,0:T(8,128)(2,1)}, u32[]{:S(2)}) copy-start(bf16[1,1024,256]{2,1,0:T(8,128)(2,1)} %param.13) | copy-start | bytes 1572868
  409.8 5.2 copy-start.21
  409.8 5.2 copy-start.23
  415.0 3.1 copy-start.3
  418.2 7.0 %copy-start.5 = (bf16[1,1024,256]{1,2,0:T(8,128)(2,1)S(1)}, bf16[1,1024,256]{1,2,0:T(8,128)(2,1)}, u32[]{:S(2)}) copy-start(bf16[1,1024,256]{1,2,0:T(8,128)(2,1)} %copy-done.4) | copy-start | bytes 1572868
  418.2 7.0 %copy-start.12 = (bf16[1024,768]{1,0:T(8,128)(2,1)S(1)}, bf16[1024,768]{1,0:T(8,128)(2,1)}, u32[]{:S(2)}) copy-start(bf16[1024,768]{1,0:T(8,128)(2,1)} %gather_fusion.3) | copy-start | bytes 4718596
  418.2 7.0 %copy-start.19 = (bf16[256,768]{1,0:T(8,128)(2,1)S(1)}, bf16[256,768]{1,0:T(8,128)(2,1)}, u32[]{:S(2)}) copy-start(bf16[256,768]{1,0:T(8,128)(2,1)} %param.14) | copy-start | bytes 1179652
  425.9 158.5 %copy-start.1 = (bf16[256,1024]{1,0:T(8,128)(2,1)S(1)}, bf16[256,1024]{1,0:T(8,128)(2,1)}, u32[]{:S(2)}) copy-start(bf16[256,1024]{1,0:T(8,128)(2,1)} %param.16) | copy-start | bytes 1572868
  577.1 6.2 %copy-start.13 = (f32[1024,256]{1,0:T(8,128)S(1)}, f32[1024,256]{1,0:T(8,128)}, u32[]{:S(2)}) copy-start(f32[1024,256]{1,0:T(8,128)} %get-tuple-element.133) | copy-start | bytes 3145732
Sparse Core Ops, SparseCore 0:
  418.3 158.7 all-reduce.2
where the time goes:
time: 598 us; the launch traced here: 591 us
  waiting for transfers between devices  249 us (42%)
  matrix products  164 us (27%)
  local copies, waits for them, and re-layouts  78.3 us (13%)
  other arithmetic  58.3 us (10%)
  starting transfers between devices  26.2 us (4%)
  between operations  14.5 us (2%)
    psum x1, waiting for transfers between devices, body(): lax.psum((weight_first, weight_out, weight_up, weight_down), ('seq', 'dp'))  149 us
    dot_general x52, matrix products, contract_last(): lax.dot_general(left, right, (((1,), (1,)), ((), ())), preferred_element_...  74.3 us
    dot_general x36, matrix products, contract_rows(): lax.dot_general(left, right, (((0,), (0,)), ((), ())), preferred_element_...  48.4 us
    all_to_all x1, waiting for transfers between devices, body(): lax.all_to_all(pack_rows(projected, slot_index, peer_count, slot_room), '...  45.1 us
    all_to_all x1, waiting for transfers between devices, body(): lax.all_to_all(gather_back(grad_ordered, places, row_count, peer_count, s...  27.7 us
    scatter x4, local copies, waits for them, and re-layouts, place_rows(): return jnp.zeros((row_count, flattened.shape[1]), flattened.dtype).at[pla...  23.6 us
    reduce_sum x32, other arithmetic, head_probs(): return raised / jnp.sum(raised, axis=-1, keepdims=True)  23.4 us
    dot_general x16, matrix products, head_backward(): jnp.dot(grad_scores, keys_head, preferred_element_type=jnp.float32) * factor  18.4 us
  transfers between devices with their start and end apart: 6, of which 5 were waited for; matrix products, arithmetic and copies ran while one was open for 6% of the time, Pallas kernels for 0%

commit v1 on v0

v1 whole, which is shorter than its diff:
```python
import math

import jax
import jax.numpy as jnp
from jax import lax
from jax.experimental import pallas as pl
from jax.experimental.pallas import tpu as pltpu
from jax.sharding import PartitionSpec as P

BF = jnp.bfloat16
F32 = jnp.float32
C = 256
HEADS = 16
DH = 16
FF = 1024
ROWS = 1024
PEERS = 16
ROOM = 128
SLOTS = PEERS * ROOM
BLK = 256
NB = ROWS // BLK
EPS = 1e-05
GELU_A = 0.7978845608028654
GELU_B = 0.044715


def dot(left, right):
    return lax.dot_general(left, right, (((1,), (0,)), ((), ())), preferred_element_type=F32)


def dot_nt(left, right):
    return lax.dot_general(left, right, (((1,), (1,)), ((), ())), preferred_element_type=F32)


def iota(shape, axis):
    return lax.broadcasted_iota(jnp.int32, shape, axis)


def one_hot(cond):
    return jnp.where(cond, 1.0, 0.0).astype(BF)


def transpose_bf(values):
    return values.astype(F32).T.astype(BF)


def normalize(values):
    center = jnp.mean(values, axis=-1, keepdims=True)
    shifted = values - center
    inverse_std = lax.rsqrt(jnp.mean(shifted * shifted, axis=-1, keepdims=True) + EPS)
    return shifted * inverse_std, inverse_std


def norm_back(normed, inverse_std, upstream):
    return inverse_std * (
        upstream
        - jnp.mean(upstream, axis=-1, keepdims=True)
        - normed * jnp.mean(upstream * normed, axis=-1, keepdims=True)
    )


def gelu_pair(inputs):
    square = inputs * inputs
    tangent = jnp.tanh(GELU_A * (inputs + GELU_B * square * inputs))
    half = 0.5 * (1.0 + tangent)
    slopes = half + 0.5 * inputs * (1.0 - tangent * tangent) * GELU_A * (
        1.0 + 3.0 * GELU_B * square
    )
    return inputs * half, slopes


def column_of(row):
    return jnp.broadcast_to(row, (128, 128)).T[:, 0:1]


def slot_rows(targets):
    owner = lax.shift_right_logical(targets, 10)
    local = jnp.bitwise_and(targets, 1023)
    marks = iota((PEERS, ROWS), 0) == owner
    before = one_hot(iota((ROWS, ROWS), 0) < iota((ROWS, ROWS), 1))
    counts = dot(one_hot(marks), before)
    rank = jnp.sum(jnp.where(marks, counts, 0.0), axis=0, keepdims=True)
    slot = owner * ROOM + rank.astype(jnp.int32)
    part = iota((PEERS, ROWS), 0)
    aux = jnp.where(
        part == 0,
        lax.shift_right_logical(local, 5),
        jnp.where(part == 1, jnp.bitwise_and(local, 31), 1),
    )
    return slot, aux.astype(F32).astype(BF)


def pack_kernel(tgt_ref, pts_ref, cot_ref, spts_ref, scot_ref, place_ref, slot_ref):
    slot, aux = slot_rows(tgt_ref[...])
    slot_ref[...] = slot
    for peer in range(PEERS):
        mine = one_hot(iota((ROOM, ROWS), 0) + peer * ROOM == slot)
        spts_ref[peer] = dot(mine, pts_ref[...]).astype(BF)
        scot_ref[peer] = dot(mine, cot_ref[...]).astype(BF)
        found = dot_nt(aux, mine)
        place = jnp.where(
            found[2:3] > 0.5, found[0:1] * 32.0 + found[1:2], float(ROWS)
        ).astype(jnp.int32)
        place_ref[peer] = jnp.broadcast_to(place, (8, ROOM))


def unpack_kernel(slot_ref, bres_ref, bgrad_ref, res_ref, grad_ref):
    back_r = bres_ref[...].reshape(SLOTS, C)
    back_g = bgrad_ref[...].reshape(SLOTS, C)
    for block in range(ROWS // 128):
        col = column_of(slot_ref[:, block * 128 : (block + 1) * 128].astype(F32))
        mine = one_hot(iota((128, SLOTS), 1) == col.astype(jnp.int32))
        rows = slice(block * 128, (block + 1) * 128)
        res_ref[rows, :] = dot(mine, back_r).astype(BF)
        grad_ref[rows, :] = dot(mine, back_g).astype(BF)


def place_rows(place_ref, recv_ref, out_ref):
    recv = recv_ref[...].reshape(SLOTS, C)

    for block in range(NB):
        pieces = [
            one_hot(iota((BLK, ROOM), 0) + block * BLK == place_ref[peer, 0:1, :])
            for peer in range(PEERS)
        ]
        out_ref[block * BLK : (block + 1) * BLK, :] = dot(
            jnp.concatenate(pieces, axis=1), recv
        ).astype(BF)


def back_rows(place_ref, rows_ref, out_ref):
    rows = rows_ref[...]
    for peer in range(PEERS):
        col = column_of(place_ref[peer, 0:1, :].astype(F32)).astype(jnp.int32)
        out_ref[peer] = dot(one_hot(iota((ROOM, ROWS), 1) == col), rows).astype(BF)


def first_part(x_ref, w_ref, s):
    normed, _ = normalize(x_ref[...].astype(F32))
    first = normed.astype(BF)
    s.first_t[...] = transpose_bf(first)
    qs = (dot(first, w_ref[:, 0:C]).astype(BF).astype(F32) * 0.25).astype(BF)
    k = dot(first, w_ref[:, C : 2 * C]).astype(BF)
    v = dot(first, w_ref[:, 2 * C : 3 * C]).astype(BF)
    s.q[...] = qs
    s.k[...] = k
    s.v[...] = v
    s.qt[...] = transpose_bf(qs)
    s.kt[...] = (k.astype(F32).T * 0.25).astype(BF)
    v_t = transpose_bf(v)
    s.vt[:, 0:DH, :] = v_t.reshape(HEADS, DH, ROWS)
    s.vt[:, DH : 2 * DH, :] = jnp.ones((HEADS, DH, ROWS), BF)
    s.zq[...] = jnp.zeros((C, ROWS), BF)


def only_head(h, zeroed_ref, rows):
    at = pl.multiple_of(h * DH, DH)
    zeroed_ref[pl.ds(pl.multiple_of(jnp.maximum(h - 1, 0) * DH, DH), DH), :] = jnp.zeros(
        (DH, ROWS), BF
    )
    zeroed_ref[pl.ds(at, DH), :] = rows
    return at


def attend(s):
    @pl.loop(0, HEADS)
    def _(h):
        at = only_head(h, s.zq, s.qt[pl.ds(pl.multiple_of(h * DH, DH), DH), :])
        values = s.vt[h]
        for block in range(NB):
            cols = slice(block * BLK, (block + 1) * BLK)
            scores = dot(s.k[...], s.zq[:, cols])
            raised = jnp.exp(scores - jnp.max(scores, axis=0, keepdims=True)).astype(BF)
            s.p[h, :, cols] = raised
            out = dot(values, raised)
            inverse = 1.0 / out[DH : DH + 1]
            s.ot[pl.ds(at, DH), cols] = (out[0:DH] * inverse).astype(BF)
            s.inv[pl.ds(h, 1), cols] = inverse


def feed_forward(s, x_ref, cot_ref, w_out, w_up, w_down, res_ref):
    @pl.loop(0, NB)
    def _(block):
        rows = pl.ds(pl.multiple_of(block * BLK, BLK), BLK)
        features = x_ref[rows, :].astype(F32)
        tile_grad = cot_ref[rows, :]
        hidden = features + dot(s.att[rows, :], w_out[...])
        normed, inverse = normalize(hidden)
        second = normed.astype(BF)
        s.second[rows, :] = second
        expanded = dot(second, w_up[...])
        activated, slopes = gelu_pair(expanded)
        activated = activated.astype(BF)
        s.act[rows, :] = activated
        res_ref[rows, :] = (hidden + dot(activated, w_down[...])).astype(BF)
        gexp = (dot_nt(tile_grad, w_down[...]) * slopes).astype(BF)
        s.gexp[rows, :] = gexp
        grad_hidden = tile_grad.astype(F32) + norm_back(normed, inverse, dot_nt(gexp, w_up[...]))
        s.gh[rows, :] = grad_hidden
        hrows = grad_hidden.astype(BF)
        s.hrows[rows, :] = hrows
        s.datt[rows, :] = dot_nt(hrows, w_out[...]).astype(BF)


def ff_grads(s, cot_ref, factor, g_out, g_up, g_down):
    g_out[...] = dot(s.ot[...], s.hrows[...]) * factor
    g_up[...] = dot(transpose_bf(s.second[...]), s.gexp[...]) * factor
    g_down[...] = dot(transpose_bf(cot_ref[...]), s.act[...]).T * factor


def attend_back(s):
    dot_t = s.datt[...].astype(F32).T
    inverse = s.inv[...].reshape(HEADS, 1, ROWS)
    don_t = (dot_t.reshape(HEADS, DH, ROWS) * inverse).astype(BF)
    inner = jnp.sum(
        don_t.astype(F32) * s.ot[...].astype(F32).reshape(HEADS, DH, ROWS), axis=1, keepdims=True
    )
    s.inner[...] = inner.reshape(HEADS, ROWS)
    s.dont[...] = don_t.reshape(C, ROWS)
    s.don[...] = transpose_bf(s.dont[...])
    s.zq[...] = jnp.zeros((C, ROWS), BF)

    @pl.loop(0, HEADS)
    def _(h):
        at = only_head(h, s.zq, s.dont[pl.ds(pl.multiple_of(h * DH, DH), DH), :])
        keys = s.kt[pl.ds(at, DH), :]
        for block in range(NB):
            cols = slice(block * BLK, (block + 1) * BLK)
            dp = dot(s.v[...], s.zq[:, cols])
            ds = (s.p[h, :, cols].astype(F32) * (dp - s.inner[pl.ds(h, 1), cols])).astype(BF)
            s.ds[:, cols] = ds
            s.dqt[pl.ds(at, DH), cols] = dot(keys, ds).astype(BF)
        mine = lax.shift_right_logical(iota((ROWS, C), 1), 4) == h
        s.dv[...] = jnp.where(mine, dot(s.p[h], s.don[...]), s.dv[...].astype(F32)).astype(BF)
        s.dk[...] = jnp.where(mine, dot(s.ds[...], s.q[...]), s.dk[...].astype(F32)).astype(BF)


def last_part(s, x_ref, w_ref, factor, g_qkv, grad_ref):
    dq = transpose_bf(s.dqt[...])
    dk = s.dk[...]
    dv = s.dv[...]
    g_first = dot_nt(dq, w_ref[:, 0:C]) + dot_nt(dk, w_ref[:, C : 2 * C])
    g_first = (g_first + dot_nt(dv, w_ref[:, 2 * C : 3 * C])).astype(BF).astype(F32)
    g_qkv[:, 0:C] = dot(s.first_t[...], dq) * factor
    g_qkv[:, C : 2 * C] = dot(s.first_t[...], dk) * factor
    g_qkv[:, 2 * C : 3 * C] = dot(s.first_t[...], dv) * factor
    normed, inverse = normalize(x_ref[...].astype(F32))
    grad_ref[...] = (s.gh[...] + norm_back(normed, inverse, g_first)).astype(BF)


class Scratch:
    shapes = dict(
        x=((ROWS, C), BF), cot=((ROWS, C), BF), first_t=((C, ROWS), BF),
        q=((ROWS, C), BF), k=((ROWS, C), BF), v=((ROWS, C), BF),
        qt=((C, ROWS), BF), kt=((C, ROWS), BF), vt=((HEADS, 2 * DH, ROWS), BF),
        zq=((C, ROWS), BF), p=((HEADS, ROWS, ROWS), BF), ot=((C, ROWS), BF),
        inv=((HEADS, ROWS), F32), att=((ROWS, C), BF), second=((ROWS, C), BF),
        act=((ROWS, FF), BF), gexp=((ROWS, FF), BF), gh=((ROWS, C), F32),
        hrows=((ROWS, C), BF), datt=((ROWS, C), BF), inner=((HEADS, ROWS), F32),
        dont=((C, ROWS), BF), don=((ROWS, C), BF),
        dqt=((C, ROWS), BF), dv=((ROWS, C), BF), dk=((ROWS, C), BF),
    )

    def __init__(self, refs):
        for name, ref in zip(self.shapes, refs):
            setattr(self, name, ref)
        self.ds = self.act
        self.out = self.att

    @classmethod
    def specs(cls):
        return [pltpu.VMEM(*v) for v in cls.shapes.values()]


def core_kernel(
    factor, rpts, rcot, place, w_qkv, w_out, w_up, w_down,
    bres, bgrad, g_qkv, g_out, g_up, g_down, *scratch,
):
    s = Scratch(scratch)
    place_rows(place, rpts, s.x)
    first_part(s.x, w_qkv, s)
    attend(s)
    place_rows(place, rcot, s.cot)
    s.att[...] = transpose_bf(s.ot[...])
    feed_forward(s, s.x, s.cot, w_out, w_up, w_down, s.out)
    back_rows(place, s.out, bres)
    ff_grads(s, s.cot, factor, g_out, g_up, g_down)
    attend_back(s)
    last_part(s, s.x, w_qkv, factor, g_qkv, s.out)
    back_rows(place, s.out, bgrad)


VM = pl.BlockSpec(memory_space=pltpu.VMEM)
LIMIT = 65000 * 1024


def call(kernel, ins, outs, scratch=()):
    return pl.pallas_call(
        kernel,
        out_shape=[jax.ShapeDtypeStruct(*o) for o in outs],
        in_specs=[VM] * len(ins),
        out_specs=[VM] * len(outs),
        scratch_shapes=list(scratch),
        compiler_params=pltpu.CompilerParams(vmem_limit_bytes=LIMIT),
    )(*ins)


SENT = ((PEERS, ROOM, C), BF)
GRADS = [((C, 3 * C), F32), ((C, C), F32), ((C, FF), F32), ((FF, C), F32)]


def exchange(values):
    return lax.all_to_all(values, "seq", split_axis=0, concat_axis=0, tiled=True)


def core(factor, rpts, rcot, place, *weights):
    return call(
        lambda *refs: core_kernel(factor, *refs),
        (rpts, rcot, place, *weights),
        [SENT, SENT, *GRADS],
        Scratch.specs(),
    )


def body(points, targets, cotangent, w_qkv, w_out, w_up, w_down):
    row_count = points.shape[1]
    factor = 1.0 / math.sqrt(
        points.shape[0] * lax.axis_size("dp") * lax.axis_size("seq") * row_count
    )
    spts, scot, place, slot = call(
        pack_kernel,
        (targets, points[0], cotangent[0]),
        [SENT, SENT, ((PEERS, 8, ROOM), jnp.int32), ((1, ROWS), jnp.int32)],
    )
    place = exchange(place)
    rpts = exchange(spts)
    rcot = exchange(scot)
    bres, bgrad, *grads = core(factor, rpts, rcot, place, w_qkv, w_out, w_up, w_down)
    result, grad_points = call(
        unpack_kernel,
        (slot, exchange(bres), exchange(bgrad)),
        [((ROWS, C), BF), ((ROWS, C), BF)],
    )
    summed = lax.psum(tuple(grads), ("seq", "dp"))
    return (result[None], grad_points[None], *summed)


def solution(mesh):
    return jax.shard_map(
        body,
        mesh=mesh,
        in_specs=(P("dp", "seq", None), P("dp", "seq"), P("dp", "seq", None), P(), P(), P(), P()),
        out_specs=(P("dp", "seq", None), P("dp", "seq", None), P(), P(), P(), P()),
        check_vma=False,
    )
```

time: 598 us -> 369 us (0.62); the launches traced: 591 us -> 369 us
  matrix products: 164 us -> 0 us
  Pallas kernels: 0 us -> 128 us
  waiting for transfers between devices: 249 us -> 148 us
  local copies, waits for them, and re-layouts: 78.3 us -> 5.46 us
  blocking collectives: 0 us -> 68.9 us
  other arithmetic: 58.3 us -> 0 us
  starting transfers between devices: 26.2 us -> 3.7 us
    dot_general x124 -> x0, matrix products: 164 us -> none  [the longest x52 74.3 us: contract_last(): lax.dot_general(left, right, (((1,), (1,)), ((), ())), preferred_element_...]
    pallas_call x0 -> x3, Pallas kernels: none -> 128 us  [call(): pl.pallas_call(kernel, out_shape=[jax.ShapeDtypeStruct(*o) for o in outs]...]
    all_to_all x5 -> x1, waiting for transfers between devices: 101 us -> 12.8 us  [exchange(): lax.all_to_all(values, 'seq', split_axis=0, concat_axis=0, tiled=True)]
    all_to_all x0 -> x4, blocking collectives: none -> 68.9 us  [exchange(): lax.all_to_all(values, 'seq', split_axis=0, concat_axis=0, tiled=True)]
    scatter x7 -> x0, local copies, waits for them, and re-layouts: 42.4 us -> none  [the longest x4 23.6 us: place_rows(): return jnp.zeros((row_count, flattened.shape[1]), flattened.dtype).at[pla...]
    reduce_sum x52 -> x0, other arithmetic: 36.3 us -> none  [the longest x32 23.4 us: head_probs(): return raised / jnp.sum(raised, axis=-1, keepdims=True)]
    gather x4 -> x0, local copies, waits for them, and re-layouts: 26.1 us -> none  [the longest x2 17 us: gather_back(): values[jnp.minimum(places, row_count - 1)]]
    all_to_all x5 -> x1, starting transfers between devices: 25.9 us -> 3.66 us  [exchange(): lax.all_to_all(values, 'seq', split_axis=0, concat_axis=0, tiled=True)]
  transfers between devices with their start and end apart: 6 -> 2, of which waited for: 5 -> 2; matrix products, arithmetic and copies ran while one was open for 6% -> 0% of each run, Pallas kernels for 0% -> 1%
where the time goes in v1:
time: 369 us
  waiting for transfers between devices  148 us (40%)
  Pallas kernels  128 us (35%)
  blocking collectives  68.9 us (19%)
  between operations  14.1 us (4%)
  local copies, waits for them, and re-layouts  5.46 us (1%)
  starting transfers between devices  3.7 us (1%)
    psum x1, waiting for transfers between devices, body(): summed = lax.psum(tuple(grads), ('seq', 'dp'))  135 us
    pallas_call x3, Pallas kernels, call(): pl.pallas_call(kernel, out_shape=[jax.ShapeDtypeStruct(*o) for o in outs]...  128 us
    all_to_all x4, blocking collectives, exchange(): lax.all_to_all(values, 'seq', split_axis=0, concat_axis=0, tiled=True)  68.9 us
    all_to_all x1, waiting for transfers between devices, exchange(): lax.all_to_all(values, 'seq', split_axis=0, concat_axis=0, tiled=True)  12.8 us
  transfers between devices with their start and end apart: 2, of which 2 were waited for; matrix products, arithmetic and copies ran while one was open for 0% of the time, Pallas kernels for 1%

profile of v1, /device:TPU:1, one launch (start us, length us, event | category | flops | bytes accessed | tf_op | source)
XLA Modules:
  0.0 368.5 jit_solution(8519361980892583202)
XLA Ops:
  7.2 6.3 %shard_map.118 = (bf16[16,128,256]{2,1,0:T(8,128)(2,1)}, bf16[16,128,256]{2,1,0:T(8,128)(2,1)}, s32[16,8,128]{2,1,0:T(8,128)}, s32[1,1024]{1,0:T(1,128)}) custom-call(s32[1,1024]{1,0:T(1,128)} %tgt_ref.1, bf16[1024,256]{1,0:T(8,128)(2,1)} %bitcast.4, bf16[1024,256]{1,0:T(8,128)(2,1)} %bitcast.5), custom_call_target="tpu_custom_call" | custom-call | tf_op jit(solution)/shard_map/pallas_call | solution.py:298
  13.4 14.2 %all_to_all.25.refs_2_ = s32[16,8,128]{2,1,0:T(8,128)} all-to-all(s32[16,8,128]{2,1,0:T(8,128)} %get-tuple-element.21), channel_id=1, replica_groups=mesh['seq'=16,'dp'=8] {'seq'}, dimensions={0} | all-to-all | bytes 131072 | tf_op jit(solution)/shard_map/all_to_all | solution.py:313
  27.6 0.0 copy-start.4
  27.6 19.9 %all_to_all.26.refs_0_ = bf16[16,128,256]{2,1,0:T(8,128)(2,1)} all-to-all(bf16[16,128,256]{2,1,0:T(8,128)(2,1)} %get-tuple-element.19), channel_id=1, replica_groups=mesh['seq'=16,'dp'=8] {'seq'}, dimensions={0} | all-to-all | bytes 2097152 | tf_op jit(solution)/shard_map/all_to_all | solution.py:313
  47.5 0.0 copy-done.4
  47.5 17.3 %all_to_all.27.refs_1_ = bf16[16,128,256]{2,1,0:T(8,128)(2,1)} all-to-all(bf16[16,128,256]{2,1,0:T(8,128)(2,1)S(1)} %copy-done.4), channel_id=1, replica_groups=mesh['seq'=16,'dp'=8] {'seq'}, dimensions={0} | all-to-all | bytes 2097152 | tf_op jit(solution)/shard_map/all_to_all | solution.py:313
  64.9 117.1 %shard_map.119 = (bf16[16,128,256]{2,1,0:T(8,128)(2,1)}, bf16[16,128,256]{2,1,0:T(8,128)(2,1)}, f32[256,768]{1,0:T(8,128)}, f32[256,256]{1,0:T(8,128)}, f32[256,1024]{1,0:T(8,128)}, /*index=5*/f32[1024,256]{1,0:T(8,128)}) custom-call(bf16[16,128,256]{2,1,0:T(8,128)(2,1)} %all_to_all.26.refs_0_, bf16[16,128,256]{2,1,0:T(8,128)(2,1)} %all_to_all.27.refs_1_, ...), custom_call_target="tpu_custom_call" | custom-call | tf_op jit(solution)/shard_map/pallas_call | solution.py:298
  182.0 3.7 all-to-all-start.3
  185.6 0.0 all-reduce.3.cloned.1.call-start
  185.7 0.0 copy-start.3
  185.7 0.7 all-reduce.3.cloned.1.call-update
  186.4 12.8 %all-to-all-done.3.bres_ref = bf16[16,128,256]{2,1,0:T(8,128)(2,1)S(1)} async-done(((bf16[16,128,256]{2,1,0:T(8,128)(2,1)}), bf16[16,128,256]{2,1,0:T(8,128)(2,1)S(1)}, u32[]{:S(2)}, u32[]{:S(2)}) %all-to-all-start.3) | async-done | bytes 1048608 | tf_op jit(solution)/shard_map/all_to_all | solution.py:313
  199.1 0.0 copy-start
  199.2 0.0 copy-done.3
  199.2 17.5 %all_to_all.28.bgrad_ref = bf16[16,128,256]{2,1,0:T(8,128)(2,1)} all-to-all(bf16[16,128,256]{2,1,0:T(8,128)(2,1)S(1)} %copy-done.3), channel_id=1, replica_groups=mesh['seq'=16,'dp'=8] {'seq'}, dimensions={0} | all-to-all | bytes 2097152 | tf_op jit(solution)/shard_map/all_to_all | solution.py:313
  216.6 0.0 copy-done
  216.6 5.0 %shard_map.120 = (bf16[1024,256]{1,0:T(8,128)(2,1)}, bf16[1024,256]{1,0:T(8,128)(2,1)}) custom-call(s32[1,1024]{1,0:T(1,128)} %get-tuple-element.18.slot_ref, bf16[16,128,256]{2,1,0:T(8,128)(2,1)} %copy-done, bf16[16,128,256]{2,1,0:T(8,128)(2,1)} %all_to_all.28.bgrad_ref), custom_call_target="tpu_custom_call" | custom-call | tf_op jit(solution)/shard_map/pallas_call | solution.py:298
  221.7 134.5 %all-reduce.3.cloned.1.call-done = (f32[256,768]{1,0:T(8,128)}, f32[256,256]{1,0:T(8,128)}, f32[256,1024]{1,0:T(8,128)}, f32[1024,256]{1,0:T(8,128)}) async-done(((f32[256,768]{1,0:T(8,128)}, f32[256,256]{1,0:T(8,128)}, f32[256,1024]{1,0:T(8,128)}, f32[1024,256]{1,0:T(8,128)}), (f32[256,768]{1,0:T(8,128)}, f32[256,256]{1,0:T(8,128)}, f32[256,1024]{1,0:T(8,128)}, ...) | async-done | bytes 3145744 | tf_op jit(solution)/shard_map/psum | solution.py:344
  356.2 0.0 copy-start.5
  356.2 0.0 copy-start.2
  356.2 2.2 copy.17
  358.4 0.0 copy-done.5
  358.4 0.7 copy.18
  359.1 0.0 copy-done.2
  359.1 0.0 copy-start.1
  359.1 1.0 copy.19
  360.1 0.6 copy-done.1
  360.7 1.0 copy.20
Async XLA Ops:
  27.6 19.9 %copy-start.4 = (bf16[16,128,256]{2,1,0:T(8,128)(2,1)S(1)}, bf16[16,128,256]{2,1,0:T(8,128)(2,1)}, u32[]{:S(2)}) copy-start(bf16[16,128,256]{2,1,0:T(8,128)(2,1)} %get-tuple-element.20) | copy-start | bytes 3145732
  182.0 17.2 %all-to-all-start.3 = ((bf16[16,128,256]{2,1,0:T(8,128)(2,1)}), bf16[16,128,256]{2,1,0:T(8,128)(2,1)S(1)}, u32[]{:S(2)}, u32[]{:S(2)}) async-start(bf16[16,128,256]{2,1,0:T(8,128)(2,1)} %get-tuple-element.22), calls=%async_computation.3 | async-start | bytes 2097152 | tf_op jit(solution)/shard_map/all_to_all | solution.py:313
  185.6 170.6 %all-reduce.3.cloned.1.call-start = ((), (), s32[]{:S(2)}) async-start(), calls=%async_computation.5 | async-start | bytes 6291456 | tf_op jit(solution)/shard_map/psum | solution.py:344
  185.7 13.5 %copy-start.3 = (bf16[16,128,256]{2,1,0:T(8,128)(2,1)S(1)}, bf16[16,128,256]{2,1,0:T(8,128)(2,1)}, u32[]{:S(2)}) copy-start(bf16[16,128,256]{2,1,0:T(8,128)(2,1)} %get-tuple-element.23) | copy-start | bytes 3145732
  199.1 17.5 %copy-start = (bf16[16,128,256]{2,1,0:T(8,128)(2,1)}, bf16[16,128,256]{2,1,0:T(8,128)(2,1)S(1)}, u32[]{:S(2)}) copy-start(bf16[16,128,256]{2,1,0:T(8,128)(2,1)S(1)} %all-to-all-done.3.bres_ref) | copy-start | bytes 3145732
  356.2 2.2 copy-start.5
  356.2 2.9 copy-start.2
  359.1 1.6 copy-start.1
Sparse Core Ops, SparseCore 0:
  192.3 163.8 all-reduce.2

commit v2 on v1

v2 whole, which is shorter than its diff:
```python
import math

import jax
import jax.numpy as jnp
from jax import lax
from jax.experimental import pallas as pl
from jax.experimental.pallas import tpu as pltpu
from jax.sharding import PartitionSpec as P

BF = jnp.bfloat16
F32 = jnp.float32
C = 256
HEADS = 16
DH = 16
FF = 1024
ROWS = 1024
PEERS = 16
ROOM = 128
SLOTS = PEERS * ROOM
BLK = 256
NB = ROWS // BLK
HALF = 128
EPS = 1e-05
GELU_A = 0.7978845608028654
GELU_B = 0.044715


def dot(left, right):
    return lax.dot_general(left, right, (((1,), (0,)), ((), ())), preferred_element_type=F32)


def dot_nt(left, right):
    return lax.dot_general(left, right, (((1,), (1,)), ((), ())), preferred_element_type=F32)


def iota(shape, axis):
    return lax.broadcasted_iota(jnp.int32, shape, axis)


def one_hot(cond):
    return jnp.where(cond, 1.0, 0.0).astype(BF)


def transpose_bf(values):
    return values.astype(F32).T.astype(BF)


def normalize(values):
    center = jnp.mean(values, axis=-1, keepdims=True)
    shifted = values - center
    inverse_std = lax.rsqrt(jnp.mean(shifted * shifted, axis=-1, keepdims=True) + EPS)
    return shifted * inverse_std, inverse_std


def norm_back(normed, inverse_std, upstream):
    return inverse_std * (
        upstream
        - jnp.mean(upstream, axis=-1, keepdims=True)
        - normed * jnp.mean(upstream * normed, axis=-1, keepdims=True)
    )


def gelu_pair(inputs):
    square = inputs * inputs
    tangent = jnp.tanh(GELU_A * (inputs + GELU_B * square * inputs))
    half = 0.5 * (1.0 + tangent)
    slopes = half + 0.5 * inputs * (1.0 - tangent * tangent) * GELU_A * (
        1.0 + 3.0 * GELU_B * square
    )
    return inputs * half, slopes


def column_of(row):
    return jnp.broadcast_to(row, (128, 128)).T[:, 0:1]


def slot_rows(targets, me):
    owner = lax.shift_right_logical(targets, 10)
    local = jnp.bitwise_and(targets, ROWS - 1)
    marks = iota((PEERS, ROWS), 0) == owner
    before = one_hot(iota((ROWS, ROWS), 0) < iota((ROWS, ROWS), 1))
    counts = dot(one_hot(marks), before)
    rank = jnp.sum(jnp.where(marks, counts, 0.0), axis=0, keepdims=True)
    slot = jnp.bitwise_and(owner - me, PEERS - 1) * ROOM + rank.astype(jnp.int32)
    part = iota((PEERS, ROWS), 0)
    aux = jnp.where(
        part == 0,
        lax.shift_right_logical(local, 5),
        jnp.where(part == 1, jnp.bitwise_and(local, 31), 1),
    )
    return slot, aux.astype(F32).astype(BF)


def home_rows(s, back, out_ref):
    rows = back[...].reshape(SLOTS, C)
    for block in range(ROWS // 128):
        at = slice(block * 128, (block + 1) * 128)
        col = column_of(s.slot[:, at].astype(F32)).astype(jnp.int32)
        out_ref[at, :] = dot(one_hot(iota((128, SLOTS), 1) == col), rows).astype(BF)


def place_rows(s, recv_ref, out_ref):
    recv = recv_ref[...].reshape(SLOTS, C)
    for block in range(NB):
        pieces = [
            one_hot(iota((BLK, ROOM), 0) + block * BLK == s.place[peer, 0:1, :])
            for peer in range(PEERS)
        ]
        out_ref[block * BLK : (block + 1) * BLK, :] = dot(
            jnp.concatenate(pieces, axis=1), recv
        ).astype(BF)


def first_part(s, w_ref):
    normed, _ = normalize(s.x[...].astype(F32))
    first = normed.astype(BF)
    s.first_t[...] = transpose_bf(first)
    qs = (dot(first, w_ref[:, 0:C]).astype(BF).astype(F32) * 0.25).astype(BF)
    k = dot(first, w_ref[:, C : 2 * C]).astype(BF)
    v = dot(first, w_ref[:, 2 * C : 3 * C]).astype(BF)
    s.q[...] = qs
    s.k[...] = k
    s.v[...] = v
    s.qt[...] = transpose_bf(qs)
    s.kt[...] = transpose_bf(k)
    for half in range(2):
        s.va[half, :, 0:HALF] = v[:, half * HALF : (half + 1) * HALF]
        s.va[half, :, HALF:C] = jnp.ones((ROWS, HALF), BF)
    s.za[...] = jnp.zeros((C, ROWS), BF)


def head_rows(h):
    return pl.ds(pl.multiple_of(h * DH, DH), DH)


def only_head(h, zeroed_ref, rows):
    zeroed_ref[head_rows(jnp.maximum(h - 1, 0)), :] = jnp.zeros((DH, ROWS), BF)
    zeroed_ref[head_rows(h), :] = rows


def attend(s):
    @pl.loop(0, HEADS)
    def _(h):
        half = h // 8
        only_head(h, s.za, s.kt[head_rows(h), :])
        lane = iota((HALF, HALF), 1)
        for block in range(ROWS // HALF):
            rows = slice(block * HALF, (block + 1) * HALF)
            scores = dot(s.q[rows, :], s.za[...])
            top = jnp.max(scores, axis=1, keepdims=True)
            out = dot(jnp.exp(scores - top).astype(BF), s.va[half])
            total = out[:, HALF : HALF + 1]
            s.heads[half, rows, :] = jnp.where(
                lax.shift_right_logical(lane, 4) == h - 8 * half,
                out[:, 0:HALF] * (1.0 / total),
                s.heads[half, rows, :],
            )
            s.lse[rows, :] = jnp.where(lane == h, top + jnp.log(total), s.lse[rows, :])


def feed_forward(s, w_out, w_up, w_down):
    @pl.loop(0, NB)
    def _(block):
        rows = pl.ds(pl.multiple_of(block * BLK, BLK), BLK)
        features = s.x[rows, :].astype(F32)
        tile_grad = s.cot[rows, :]
        hidden = features + dot(s.att[rows, :], w_out[...])
        normed, inverse = normalize(hidden)
        second = normed.astype(BF)
        s.second[rows, :] = second
        expanded = dot(second, w_up[...])
        activated, slopes = gelu_pair(expanded)
        activated = activated.astype(BF)
        s.act[rows, :] = activated
        s.out[rows, :] = (hidden + dot(activated, w_down[...])).astype(BF)
        gexp = (dot_nt(tile_grad, w_down[...]) * slopes).astype(BF)
        s.gexp[rows, :] = gexp
        grad_hidden = tile_grad.astype(F32) + norm_back(normed, inverse, dot_nt(gexp, w_up[...]))
        s.gh[rows, :] = grad_hidden
        hrows = grad_hidden.astype(BF)
        s.hrows[rows, :] = hrows
        s.datt[rows, :] = dot_nt(hrows, w_out[...]).astype(BF)


def attend_back(s, steps):
    dot_t = s.datt[...].astype(F32).T
    s.dot_t[...] = dot_t.astype(BF)
    inner = (dot_t * s.ot[...].astype(F32)).reshape(HEADS, DH, ROWS)
    s.inner[...] = jnp.sum(inner, axis=1, keepdims=True).reshape(HEADS, ROWS)
    s.lse_t[...] = s.lse[...].T[0:HEADS]
    s.za[...] = jnp.zeros((C, ROWS), BF)
    s.zb[...] = jnp.zeros((C, ROWS), BF)

    @pl.loop(0, HEADS)
    def _(h):
        for when, step in steps.items():
            pl.when(h == when)(step)
        only_head(h, s.za, s.qt[head_rows(h), :])
        only_head(h, s.zb, s.dot_t[head_rows(h), :])
        keys = s.kt[head_rows(h), :]
        for block in range(NB):
            cols = slice(block * BLK, (block + 1) * BLK)
            probs = jnp.exp(dot(s.k[...], s.za[:, cols]) - s.lse_t[pl.ds(h, 1), cols])
            dp = dot(s.v[...], s.zb[:, cols])
            ds = (probs * (dp - s.inner[pl.ds(h, 1), cols])).astype(BF)
            s.p[:, cols] = probs.astype(BF)
            s.ds[:, cols] = ds
            s.dqt[head_rows(h), cols] = (dot(keys, ds) * 0.25).astype(BF)
        mine = lax.shift_right_logical(iota((ROWS, C), 1), 4) == h
        s.dv[...] = jnp.where(mine, dot(s.p[...], s.datt[...]), s.dv[...])
        s.dk[...] = jnp.where(mine, dot(s.ds[...], s.q[...]), s.dk[...])


class Copies:
    def __init__(self, axis, size, me, sign, source, target, send, recv):
        self.parts = {}
        for d in range(1, size):
            peer = lax.rem(me + (d if sign > 0 else size - d), size)
            self.parts[d] = pltpu.make_async_remote_copy(
                src_ref=source(d, peer),
                dst_ref=target(d),
                send_sem=send.at[d],
                recv_sem=recv.at[d],
                device_id={axis: peer},
                device_id_type=pl.DeviceIdType.MESH,
            )

    def start(self, d=None):
        for key, part in self.parts.items():
            if d is None or key == d:
                part.start()

    def arrived(self):
        for part in self.parts.values():
            part.wait_recv()

    def sent(self):
        for part in self.parts.values():
            part.wait_send()


class Reduction:
    def __init__(self, s, name, seq, zed, n_dp, split):
        self.seq, self.zed, self.n_dp, self.split = seq, zed, n_dp, split
        self.own, self.got, self.cut, self.cut_got, self.fin, self.all = (
            getattr(s, name + part) for part in ("own", "got", "cut", "cutgot", "fin", "all")
        )
        sems = [(getattr(s, f"{name}send{i}"), getattr(s, f"{name}recv{i}")) for i in range(4)]
        self.first = lambda: Copies(
            "dp", n_dp, zed, 1, lambda d, p: self.own.at[p], lambda d: self.got.at[d], *sems[0]
        )
        self.second = lambda: Copies(
            "seq", PEERS, seq, 1, lambda d, p: self.cut.at[p], lambda d: self.cut_got.at[d], *sems[1]
        )
        self.third = lambda: Copies(
            "seq", PEERS, seq, 1, lambda d, p: self.fin.at[seq], lambda d: self.fin.at[seq], *sems[2]
        )
        self.fourth = lambda: Copies(
            "dp", n_dp, zed, 1, lambda d, p: self.all.at[zed], lambda d: self.all.at[zed], *sems[3]
        )

    def spots(self):
        rows, cols = self.cut.shape[1:]
        for piece in range(PEERS):
            up, along = (piece // 8, piece % 8) if self.split else (0, piece)
            yield piece, slice(up * rows, (up + 1) * rows), slice(along * cols, (along + 1) * cols)

    def step0(self):
        self.first().start()

    def step1(self):
        self.first().arrived()
        for piece, rows, cols in self.spots():
            total = self.own[self.zed, rows, cols].astype(F32)
            for d in range(1, self.n_dp):
                total = total + self.got[d, rows, cols].astype(F32)
            self.cut[piece] = total
        self.second().start()

    def step2(self):
        self.second().arrived()
        total = self.cut[self.seq]
        for d in range(1, PEERS):
            total = total + self.cut_got[d]
        self.fin[self.seq] = total.astype(BF)
        self.third().start()

    def step3(self):
        self.third().arrived()
        for piece, rows, cols in self.spots():
            self.all[self.zed, rows, cols] = self.fin[piece]
        self.fourth().start()

    def step4(self, out_ref):
        self.fourth().arrived()
        out_ref[...] = self.all[...].reshape(out_ref.shape)
        for copies in (self.first, self.second, self.third, self.fourth):
            copies().sent()


def scratch_of(n_dp):
    rows = C // n_dp
    room, tall, flat, sent = (PEERS, ROOM, C), (ROWS, C), (C, ROWS), pltpu.SemaphoreType.DMA
    names = {}
    for name in ("x", "cot", "q", "k", "v", "att", "second", "hrows", "datt", "out"):
        names[name] = pltpu.VMEM(tall, BF)
    for name in ("gh", "dv", "dk"):
        names[name] = pltpu.VMEM(tall, F32)
    for name in ("first_t", "qt", "kt", "za", "zb", "ot", "dot_t", "dqt"):
        names[name] = pltpu.VMEM(flat, BF)
    for name in ("act", "gexp", "p", "ds"):
        names[name] = pltpu.VMEM((ROWS, FF), BF)
    for name in ("inner", "lse_t"):
        names[name] = pltpu.VMEM((HEADS, ROWS), F32)
    names["lse"] = pltpu.VMEM((ROWS, HALF), F32)
    names["va"] = pltpu.VMEM((2, ROWS, C), BF)
    names["heads"] = pltpu.VMEM((2, ROWS, HALF), F32)
    names["slot"] = pltpu.VMEM((1, ROWS), jnp.int32)
    for name in ("place", "splace"):
        names[name] = pltpu.VMEM((PEERS, 8, ROOM), jnp.int32)
    for name in ("spts", "scot", "sres", "sgrad", "rpts", "rcot", "rres", "rgrad"):
        names[name] = pltpu.VMEM(room, BF)
    for name in ("place", "pts", "cot", "res", "grad"):
        names["send" + name] = sent((PEERS,))
        names["recv" + name] = sent((PEERS,))
    for name, wide, piece in (("a", 2 * FF, (rows, HALF)), ("b", 4 * C, (rows // 2, HALF))):
        for part in ("own", "got", "all"):
            names[name + part] = pltpu.VMEM((n_dp, rows, wide), BF)
        for part in ("cut", "cutgot"):
            names[name + part] = pltpu.VMEM((PEERS, *piece), F32)
        names[name + "fin"] = pltpu.VMEM((PEERS, *piece), BF)
        for step in range(4):
            names[f"{name}send{step}"] = sent((PEERS,))
            names[f"{name}recv{step}"] = sent((PEERS,))
    return names


class Scratch:
    def __init__(self, names, refs):
        for name, ref in zip(names, refs):
            setattr(self, name, ref)


def kernel(
    n_dp, names, tgt, pts, cot, w_qkv, w_out, w_up, w_down,
    res_out, grad_out, a_out, b_out, *refs,
):
    s = Scratch(names, refs)
    seq, zed = lax.axis_index("seq"), lax.axis_index("dp")
    barrier = pltpu.get_barrier_semaphore()
    for axis, size, me in (("seq", PEERS, seq), ("dp", n_dp, zed)):
        for d in range(1, size):
            pl.semaphore_signal(
                barrier,
                inc=1,
                device_id={axis: lax.rem(me + d, size)},
                device_id_type=pl.DeviceIdType.MESH,
            )

    def exchange(name, sign, source, target):
        return Copies(
            "seq", PEERS, seq, sign, lambda d, p: source.at[d], lambda d: target.at[d],
            getattr(s, "send" + name), getattr(s, "recv" + name),
        )

    go_place = exchange("place", 1, s.splace, s.place)
    go_pts = exchange("pts", 1, s.spts, s.rpts)
    go_cot = exchange("cot", 1, s.scot, s.rcot)
    go_res = exchange("res", -1, s.sres, s.rres)
    go_grad = exchange("grad", -1, s.sgrad, s.rgrad)

    slot, aux = slot_rows(tgt[...], seq)
    s.slot[...] = slot
    pl.semaphore_wait(barrier, PEERS - 1 + n_dp - 1)
    for d in [*range(1, PEERS), 0]:
        mine = one_hot(iota((ROOM, ROWS), 0) + d * ROOM == slot)
        found = dot_nt(aux, mine)
        place = jnp.where(
            found[2:3] > 0.5, found[0:1] * 32.0 + found[1:2], float(ROWS)
        ).astype(jnp.int32)
        place = jnp.broadcast_to(place, (8, ROOM))
        block = dot(mine, pts[...]).astype(BF)
        if d:
            s.splace[d] = place
            s.spts[d] = block
            go_place.start(d)
            go_pts.start(d)
        else:
            s.place[0] = place
            s.rpts[0] = block
    for d in [*range(1, PEERS), 0]:
        mine = one_hot(iota((ROOM, ROWS), 0) + d * ROOM == slot)
        block = dot(mine, cot[...]).astype(BF)
        if d:
            s.scot[d] = block
            go_cot.start(d)
        else:
            s.rcot[0] = block

    def send_back(go, rows_ref, mine_ref, theirs_ref):
        rows = rows_ref[...]
        for d in [*range(1, PEERS), 0]:
            col = column_of(s.place[d, 0:1, :].astype(F32)).astype(jnp.int32)
            block = dot(one_hot(iota((ROOM, ROWS), 1) == col), rows).astype(BF)
            if d:
                theirs_ref[d] = block
                go.start(d)
            else:
                mine_ref[0] = block

    go_place.arrived()
    go_pts.arrived()
    place_rows(s, s.rpts, s.x)
    first_part(s, w_qkv)
    attend(s)
    for half in range(2):
        s.att[:, half * HALF : (half + 1) * HALF] = s.heads[half].astype(BF)
    s.ot[...] = transpose_bf(s.att[...])
    go_cot.arrived()
    place_rows(s, s.rcot, s.cot)
    feed_forward(s, w_out, w_up, w_down)
    send_back(go_res, s.out, s.rres, s.sres)

    wide = Reduction(s, "a", seq, zed, n_dp, False)
    last = Reduction(s, "b", seq, zed, n_dp, True)

    def put(ref, values, at):
        ref[:, :, at : at + values.shape[1]] = values.astype(BF).reshape(
            n_dp, C // n_dp, values.shape[1]
        )

    put(s.aown, dot(transpose_bf(s.second[...]), s.gexp[...]), 0)
    put(s.aown, dot(transpose_bf(s.cot[...]), s.act[...]), FF)
    wide.step0()
    put(s.bown, dot(s.ot[...], s.hrows[...]), 3 * C)
    attend_back(s, {5: wide.step1, 8: wide.step2, 10: wide.step3})

    dq = transpose_bf(s.dqt[...])
    dk = s.dk[...].astype(BF)
    dv = s.dv[...].astype(BF)
    put(s.bown, dot(s.first_t[...], dq), 0)
    put(s.bown, dot(s.first_t[...], dk), C)
    put(s.bown, dot(s.first_t[...], dv), 2 * C)
    last.step0()
    g_first = dot_nt(dq, w_qkv[:, 0:C]) + dot_nt(dk, w_qkv[:, C : 2 * C])
    g_first = (g_first + dot_nt(dv, w_qkv[:, 2 * C : 3 * C])).astype(BF).astype(F32)
    normed, inverse = normalize(s.x[...].astype(F32))
    s.out[...] = (s.gh[...] + norm_back(normed, inverse, g_first)).astype(BF)
    send_back(go_grad, s.out, s.rgrad, s.sgrad)
    last.step1()
    go_res.arrived()
    home_rows(s, s.rres, res_out)
    last.step2()
    wide.step4(a_out)
    last.step3()
    go_grad.arrived()
    home_rows(s, s.rgrad, grad_out)
    last.step4(b_out)
    for go in (go_place, go_pts, go_cot, go_res, go_grad):
        go.sent()


def body(points, targets, cotangent, w_qkv, w_out, w_up, w_down):
    n_dp = lax.axis_size("dp")
    factor = 1.0 / math.sqrt(points.shape[0] * n_dp * lax.axis_size("seq") * points.shape[1])
    names = scratch_of(n_dp)
    vmem = pl.BlockSpec(memory_space=pltpu.VMEM)
    result, grad_points, wide, last = pl.pallas_call(
        lambda *refs: kernel(n_dp, list(names), *refs),
        out_shape=[
            jax.ShapeDtypeStruct((ROWS, C), BF),
            jax.ShapeDtypeStruct((ROWS, C), BF),
            jax.ShapeDtypeStruct((C, 2 * FF), BF),
            jax.ShapeDtypeStruct((C, 4 * C), BF),
        ],
        in_specs=[vmem] * 7,
        out_specs=[vmem] * 4,
        scratch_shapes=list(names.values()),
        compiler_params=pltpu.CompilerParams(
            vmem_limit_bytes=60 * 1024 * 1024, collective_id=0, has_side_effects=True
        ),
    )(targets, points[0], cotangent[0], w_qkv, w_out, w_up, w_down)
    wide = wide.astype(F32) * factor
    last = last.astype(F32) * factor
    return (
        result[None],
        grad_points[None],
        last[:, 0 : 3 * C],
        last[:, 3 * C :],
        wide[:, 0:FF],
        wide[:, FF:].T,
    )


def solution(mesh):
    return jax.shard_map(
        body,
        mesh=mesh,
        in_specs=(P("dp", "seq", None), P("dp", "seq"), P("dp", "seq", None), P(), P(), P(), P()),
        out_specs=(P("dp", "seq", None), P("dp", "seq", None), P(), P(), P(), P()),
        check_vma=False,
    )
```

time: 369 us -> 167 us (0.45)
  waiting for transfers between devices: 148 us -> 0 us
  blocking collectives: 68.9 us -> 0 us
  Pallas kernels: 128 us -> 158 us
  between operations: 14.1 us -> 0.66 us
  starting transfers between devices: 3.7 us -> 0 us
    psum x1 -> x0, waiting for transfers between devices: 135 us -> none  [body(): summed = lax.psum(tuple(grads), ('seq', 'dp'))]
    all_to_all x4 -> x0, blocking collectives: 68.9 us -> none  [exchange(): lax.all_to_all(values, 'seq', split_axis=0, concat_axis=0, tiled=True)]
    pallas_call x3 -> x1, Pallas kernels: 128 us -> 158 us  [body(): pl.pallas_call(lambda *refs: kernel(n_dp, list(names), *refs), out_shape=...]
    all_to_all x1 -> x0, waiting for transfers between devices: 12.8 us -> none  [exchange(): lax.all_to_all(values, 'seq', split_axis=0, concat_axis=0, tiled=True)]
  transfers between devices with their start and end apart: 2 -> 0, of which waited for: 2 -> 0; matrix products, arithmetic and copies ran while one was open for 0% -> 0% of each run, Pallas kernels for 1% -> 0%
where the time goes in v2:
time: 167 us; the launch traced here: 166 us
  Pallas kernels  158 us (95%)
  local copies, waits for them, and re-layouts  5.73 us (3%)
    pallas_call x1, Pallas kernels, body(): pl.pallas_call(lambda *refs: kernel(n_dp, list(names), *refs), out_shape=...  158 us

profile of v2, /device:TPU:1, one launch (start us, length us, event | category | flops | bytes accessed | tf_op | source)
XLA Modules:
  0.0 166.4 jit_solution(10988190736409200153)
XLA Ops:
  0.6 158.4 %shard_map.118 = (bf16[1024,256]{1,0:T(8,128)(2,1)}, bf16[1024,256]{1,0:T(8,128)(2,1)}, bf16[256,2048]{1,0:T(8,128)(2,1)}, bf16[256,1024]{1,0:T(8,128)(2,1)}) custom-call(s32[1,1024]{1,0:T(1,128)} %refs_0_.1, bf16[1024,256]{1,0:T(8,128)(2,1)} %bitcast.6, bf16[1024,256]{1,0:T(8,128)(2,1)} %bitcast.7, bf16[256,768]{1,0:T(8,128)(2,1)} %refs_3_.1, ...), custom_call_target="tpu_custom_call" | custom-call | tf_op jit(solution)/shard_map/pallas_call | solution.py:468
  159.1 1.5 convert_multiply_fusion
  160.5 1.2 slice_bitcast_fusion
  161.7 0.0 copy-start
  161.7 1.3 copy.13
  163.0 0.0 copy-start.2
  163.0 0.0 copy-done
  163.0 0.0 copy-start.1
  163.0 0.1 convert_multiply_fusion.1
  163.1 0.9 slice.16
  164.1 0.7 slice.17
  164.8 0.0 copy-done.2
  164.8 0.8 copy.16
  165.6 0.0 copy-done.1
  165.6 0.8 copy.17
Async XLA Ops:
  161.7 1.3 copy-start
  163.0 1.8 %copy-start.2 = (bf16[1024,256]{1,0:T(8,128)(2,1)S(1)}, bf16[1024,256]{1,0:T(8,128)(2,1)}, u32[]{:S(2)}) copy-start(bf16[1024,256]{1,0:T(8,128)(2,1)} %get-tuple-element.10) | copy-start | bytes 1572868
  163.0 2.6 %copy-start.1 = (bf16[1024,256]{1,0:T(8,128)(2,1)S(1)}, bf16[1024,256]{1,0:T(8,128)(2,1)}, u32[]{:S(2)}) copy-start(bf16[1024,256]{1,0:T(8,128)(2,1)} %get-tuple-element.11) | copy-start | bytes 1572868

commit v3 on v2

--- a/solution.py
+++ b/solution.py
@@ -139,7 +139,7 @@
 
 
 def attend(s):
-    @pl.loop(0, HEADS)
+    @pl.loop(0, HEADS, unroll=2)
     def _(h):
         half = h // 8
         only_head(h, s.za, s.kt[head_rows(h), :])
@@ -182,7 +182,7 @@
         s.datt[rows, :] = dot_nt(hrows, w_out[...]).astype(BF)
 
 
-def attend_back(s, steps):
+def prepare_back(s):
     dot_t = s.datt[...].astype(F32).T
     s.dot_t[...] = dot_t.astype(BF)
     inner = (dot_t * s.ot[...].astype(F32)).reshape(HEADS, DH, ROWS)
@@ -191,24 +191,31 @@
     s.za[...] = jnp.zeros((C, ROWS), BF)
     s.zb[...] = jnp.zeros((C, ROWS), BF)
 
-    @pl.loop(0, HEADS)
-    def _(h):
+
+def attend_back(s, steps):
+    @pl.loop(0, HEADS // 2)
+    def _(pair):
         for when, step in steps.items():
-            pl.when(h == when)(step)
-        only_head(h, s.za, s.qt[head_rows(h), :])
-        only_head(h, s.zb, s.dot_t[head_rows(h), :])
-        keys = s.kt[head_rows(h), :]
-        for block in range(NB):
-            cols = slice(block * BLK, (block + 1) * BLK)
-            probs = jnp.exp(dot(s.k[...], s.za[:, cols]) - s.lse_t[pl.ds(h, 1), cols])
-            dp = dot(s.v[...], s.zb[:, cols])
-            ds = (probs * (dp - s.inner[pl.ds(h, 1), cols])).astype(BF)
-            s.p[:, cols] = probs.astype(BF)
-            s.ds[:, cols] = ds
-            s.dqt[head_rows(h), cols] = (dot(keys, ds) * 0.25).astype(BF)
-        mine = lax.shift_right_logical(iota((ROWS, C), 1), 4) == h
-        s.dv[...] = jnp.where(mine, dot(s.p[...], s.datt[...]), s.dv[...])
-        s.dk[...] = jnp.where(mine, dot(s.ds[...], s.q[...]), s.dk[...])
+            pl.when(pair == when)(step)
+        for odd in range(2):
+            head_back(s, pair * 2 + odd)
+
+
+def head_back(s, h):
+    only_head(h, s.za, s.qt[head_rows(h), :])
+    only_head(h, s.zb, s.dot_t[head_rows(h), :])
+    keys = s.kt[head_rows(h), :]
+    for block in range(NB):
+        cols = slice(block * BLK, (block + 1) * BLK)
+        probs = jnp.exp(dot(s.k[...], s.za[:, cols]) - s.lse_t[pl.ds(h, 1), cols])
+        dp = dot(s.v[...], s.zb[:, cols])
+        ds = (probs * (dp - s.inner[pl.ds(h, 1), cols])).astype(BF)
+        s.p[:, cols] = probs.astype(BF)
+        s.ds[:, cols] = ds
+        s.dqt[head_rows(h), cols] = (dot(keys, ds) * 0.25).astype(BF)
+    mine = lax.shift_right_logical(iota((ROWS, C), 1), 4) == h
+    s.dv[...] = jnp.where(mine, dot(s.p[...], s.datt[...]), s.dv[...])
+    s.dk[...] = jnp.where(mine, dot(s.ds[...], s.q[...]), s.dk[...])
 
 
 class Copies:
@@ -240,8 +247,8 @@
 
 
 class Reduction:
-    def __init__(self, s, name, seq, zed, n_dp, split):
-        self.seq, self.zed, self.n_dp, self.split = seq, zed, n_dp, split
+    def __init__(self, s, name, seq, zed, n_dp):
+        self.seq, self.zed, self.n_dp = seq, zed, n_dp
         self.own, self.got, self.cut, self.cut_got, self.fin, self.all = (
             getattr(s, name + part) for part in ("own", "got", "cut", "cutgot", "fin", "all")
         )
@@ -261,8 +268,9 @@
 
     def spots(self):
         rows, cols = self.cut.shape[1:]
+        across = self.own.shape[2] // cols
         for piece in range(PEERS):
-            up, along = (piece // 8, piece % 8) if self.split else (0, piece)
+            up, along = piece // across, piece % across
             yield piece, slice(up * rows, (up + 1) * rows), slice(along * cols, (along + 1) * cols)
 
     def step0(self):
@@ -282,13 +290,17 @@
         total = self.cut[self.seq]
         for d in range(1, PEERS):
             total = total + self.cut_got[d]
-        self.fin[self.seq] = total.astype(BF)
+        self.fin[self.seq] = total
         self.third().start()
 
     def step3(self):
         self.third().arrived()
-        for piece, rows, cols in self.spots():
-            self.all[self.zed, rows, cols] = self.fin[piece]
+        across = self.own.shape[2] // self.cut.shape[2]
+        bands = [
+            jnp.concatenate([self.fin[at + piece] for piece in range(across)], axis=1)
+            for at in range(0, PEERS, across)
+        ]
+        self.all[self.zed] = jnp.concatenate(bands, axis=0).astype(BF)
         self.fourth().start()
 
     def step4(self, out_ref):
@@ -302,7 +314,7 @@
     rows = C // n_dp
     room, tall, flat, sent = (PEERS, ROOM, C), (ROWS, C), (C, ROWS), pltpu.SemaphoreType.DMA
     names = {}
-    for name in ("x", "cot", "q", "k", "v", "att", "second", "hrows", "datt", "out"):
+    for name in ("x", "cot", "dq", "q", "k", "v", "att", "second", "hrows", "datt", "out"):
         names[name] = pltpu.VMEM(tall, BF)
     for name in ("gh", "dv", "dk"):
         names[name] = pltpu.VMEM(tall, F32)
@@ -323,12 +335,15 @@
     for name in ("place", "pts", "cot", "res", "grad"):
         names["send" + name] = sent((PEERS,))
         names["recv" + name] = sent((PEERS,))
-    for name, wide, piece in (("a", 2 * FF, (rows, HALF)), ("b", 4 * C, (rows // 2, HALF))):
+    for name, wide, piece in (
+        ("a", 2 * FF, (rows, HALF)),
+        ("b", 2 * C, (rows // 4, HALF)),
+        ("c", 2 * C, (rows // 4, HALF)),
+    ):
         for part in ("own", "got", "all"):
             names[name + part] = pltpu.VMEM((n_dp, rows, wide), BF)
-        for part in ("cut", "cutgot"):
+        for part in ("cut", "cutgot", "fin"):
             names[name + part] = pltpu.VMEM((PEERS, *piece), F32)
-        names[name + "fin"] = pltpu.VMEM((PEERS, *piece), BF)
         for step in range(4):
             names[f"{name}send{step}"] = sent((PEERS,))
             names[f"{name}recv{step}"] = sent((PEERS,))
@@ -343,7 +358,7 @@
 
 def kernel(
     n_dp, names, tgt, pts, cot, w_qkv, w_out, w_up, w_down,
-    res_out, grad_out, a_out, b_out, *refs,
+    res_out, grad_out, a_out, b_out, c_out, *refs,
 ):
     s = Scratch(names, refs)
     seq, zed = lax.axis_index("seq"), lax.axis_index("dp")
@@ -372,41 +387,48 @@
     slot, aux = slot_rows(tgt[...], seq)
     s.slot[...] = slot
     pl.semaphore_wait(barrier, PEERS - 1 + n_dp - 1)
-    for d in [*range(1, PEERS), 0]:
-        mine = one_hot(iota((ROOM, ROWS), 0) + d * ROOM == slot)
-        found = dot_nt(aux, mine)
-        place = jnp.where(
+    def pack(rows_ref, own_ref, sent_ref, go):
+        for d in (4, 8, 12, 0):
+            mine = one_hot(iota((4 * ROOM, ROWS), 0) + d * ROOM == slot)
+            block = dot(mine, rows_ref[...]).astype(BF)
+            for at in range(4):
+                piece = block[at * ROOM : (at + 1) * ROOM]
+                if d + at:
+                    sent_ref[d + at] = piece
+                    go.start(d + at)
+                else:
+                    own_ref[0] = piece
+
+    pack(pts, s.rpts, s.spts, go_pts)
+    for d in (4, 8, 12, 0):
+        found = dot_nt(aux, one_hot(iota((4 * ROOM, ROWS), 0) + d * ROOM == slot))
+        places = jnp.where(
             found[2:3] > 0.5, found[0:1] * 32.0 + found[1:2], float(ROWS)
         ).astype(jnp.int32)
-        place = jnp.broadcast_to(place, (8, ROOM))
-        block = dot(mine, pts[...]).astype(BF)
-        if d:
-            s.splace[d] = place
-            s.spts[d] = block
-            go_place.start(d)
-            go_pts.start(d)
-        else:
-            s.place[0] = place
-            s.rpts[0] = block
-    for d in [*range(1, PEERS), 0]:
-        mine = one_hot(iota((ROOM, ROWS), 0) + d * ROOM == slot)
-        block = dot(mine, cot[...]).astype(BF)
-        if d:
-            s.scot[d] = block
-            go_cot.start(d)
-        else:
-            s.rcot[0] = block
+        for at in range(4):
+            place = jnp.broadcast_to(places[:, at * ROOM : (at + 1) * ROOM], (8, ROOM))
+            if d + at:
+                s.splace[d + at] = place
+                go_place.start(d + at)
+            else:
+                s.place[0] = place
+    pack(cot, s.rcot, s.scot, go_cot)
 
     def send_back(go, rows_ref, mine_ref, theirs_ref):
         rows = rows_ref[...]
-        for d in [*range(1, PEERS), 0]:
-            col = column_of(s.place[d, 0:1, :].astype(F32)).astype(jnp.int32)
-            block = dot(one_hot(iota((ROOM, ROWS), 1) == col), rows).astype(BF)
-            if d:
-                theirs_ref[d] = block
-                go.start(d)
-            else:
-                mine_ref[0] = block
+        for d in (4, 8, 12, 0):
+            cols = [
+                column_of(s.place[d + at, 0:1, :].astype(F32)).astype(jnp.int32) for at in range(4)
+            ]
+            mine = one_hot(iota((4 * ROOM, ROWS), 1) == jnp.concatenate(cols, axis=0))
+            block = dot(mine, rows).astype(BF)
+            for at in range(4):
+                piece = block[at * ROOM : (at + 1) * ROOM]
+                if d + at:
+                    theirs_ref[d + at] = piece
+                    go.start(d + at)
+                else:
+                    mine_ref[0] = piece
 
     go_place.arrived()
     go_pts.arrived()
@@ -421,8 +443,7 @@
     feed_forward(s, w_out, w_up, w_down)
     send_back(go_res, s.out, s.rres, s.sres)
 
-    wide = Reduction(s, "a", seq, zed, n_dp, False)
-    last = Reduction(s, "b", seq, zed, n_dp, True)
+    wide, early, late = (Reduction(s, name, seq, zed, n_dp) for name in "abc")
 
     def put(ref, values, at):
         ref[:, :, at : at + values.shape[1]] = values.astype(BF).reshape(
@@ -432,32 +453,72 @@
     put(s.aown, dot(transpose_bf(s.second[...]), s.gexp[...]), 0)
     put(s.aown, dot(transpose_bf(s.cot[...]), s.act[...]), FF)
     wide.step0()
-    put(s.bown, dot(s.ot[...], s.hrows[...]), 3 * C)
-    attend_back(s, {5: wide.step1, 8: wide.step2, 10: wide.step3})
-
-    dq = transpose_bf(s.dqt[...])
-    dk = s.dk[...].astype(BF)
-    dv = s.dv[...].astype(BF)
-    put(s.bown, dot(s.first_t[...], dq), 0)
-    put(s.bown, dot(s.first_t[...], dk), C)
-    put(s.bown, dot(s.first_t[...], dv), 2 * C)
-    last.step0()
-    g_first = dot_nt(dq, w_qkv[:, 0:C]) + dot_nt(dk, w_qkv[:, C : 2 * C])
-    g_first = (g_first + dot_nt(dv, w_qkv[:, 2 * C : 3 * C])).astype(BF).astype(F32)
+    out_grad = dot(s.ot[...], s.hrows[...])
+    put(s.bown, out_grad[:, 0:HALF], 3 * HALF)
+    put(s.cown, out_grad[:, HALF:C], 3 * HALF)
+
+    def put_heads(ref, half):
+        at = slice(half * HALF, (half + 1) * HALF)
+        s.dq[:, at] = transpose_bf(s.dqt[at, :])
+        for part, rows in enumerate((s.dq[:, at], s.dk[:, at].astype(BF), s.dv[:, at].astype(BF))):
+            put(ref, dot(s.first_t[...], rows), part * HALF)
+
+    prepare_back(s)
+
+    def half_way():
+        put_heads(s.bown, 0)
+        early.step0()
+        wide.step3()
+
+    attend_back(
+        s,
+        {
+            2: wide.step1,
+            3: wide.step2,
+            4: half_way,
+            5: early.step1,
+            6: early.step2,
+            7: early.step3,
+        },
+    )
+    put_heads(s.cown, 1)
+    late.step0()
+    g_first = dot_nt(s.dq[...], w_qkv[:, 0:C]) + dot_nt(s.dk[...].astype(BF), w_qkv[:, C : 2 * C])
+    g_first = g_first + dot_nt(s.dv[...].astype(BF), w_qkv[:, 2 * C : 3 * C])
     normed, inverse = normalize(s.x[...].astype(F32))
+    g_first = g_first.astype(BF).astype(F32)
     s.out[...] = (s.gh[...] + norm_back(normed, inverse, g_first)).astype(BF)
+    go_res.sent()
     send_back(go_grad, s.out, s.rgrad, s.sgrad)
-    last.step1()
+    late.step1()
     go_res.arrived()
     home_rows(s, s.rres, res_out)
-    last.step2()
+    late.step2()
     wide.step4(a_out)
-    last.step3()
+    late.step3()
+    early.step4(b_out)
     go_grad.arrived()
     home_rows(s, s.rgrad, grad_out)
-    last.step4(b_out)
-    for go in (go_place, go_pts, go_cot, go_res, go_grad):
+    late.step4(c_out)
+    for go in (go_place, go_pts, go_cot, go_grad):
         go.sent()
+
+
+def finish_kernel(factor, res, grad, a, b, c, res_out, grad_out, g_qkv, g_out, g_up, g_down, sems):
+    first = pltpu.make_async_copy(res, res_out, sems.at[0])
+    second = pltpu.make_async_copy(grad, grad_out, sems.at[1])
+    first.start()
+    second.start()
+    g_up[...] = a[:, 0:FF].astype(F32) * factor
+    for at in range(0, FF, C):
+        g_down[at : at + C, :] = a[:, FF + at : FF + at + C].astype(F32).T * factor
+    for half, ref in enumerate((b, c)):
+        for part in range(3):
+            at = part * C + half * HALF
+            g_qkv[:, at : at + HALF] = ref[:, part * HALF : (part + 1) * HALF].astype(F32) * factor
+        g_out[:, half * HALF : (half + 1) * HALF] = ref[:, 3 * HALF :].astype(F32) * factor
+    first.wait()
+    second.wait()
 
 
 def body(points, targets, cotangent, w_qkv, w_out, w_up, w_down):
@@ -465,31 +526,39 @@
     factor = 1.0 / math.sqrt(points.shape[0] * n_dp * lax.axis_size("seq") * points.shape[1])
     names = scratch_of(n_dp)
     vmem = pl.BlockSpec(memory_space=pltpu.VMEM)
-    result, grad_points, wide, last = pl.pallas_call(
+    rows_type = jax.ShapeDtypeStruct((ROWS, C), BF)
+    gathered = pl.pallas_call(
         lambda *refs: kernel(n_dp, list(names), *refs),
         out_shape=[
-            jax.ShapeDtypeStruct((ROWS, C), BF),
-            jax.ShapeDtypeStruct((ROWS, C), BF),
+            rows_type,
+            rows_type,
             jax.ShapeDtypeStruct((C, 2 * FF), BF),
-            jax.ShapeDtypeStruct((C, 4 * C), BF),
+            jax.ShapeDtypeStruct((C, 2 * C), BF),
+            jax.ShapeDtypeStruct((C, 2 * C), BF),
         ],
         in_specs=[vmem] * 7,
-        out_specs=[vmem] * 4,
+        out_specs=[vmem] * 5,
         scratch_shapes=list(names.values()),
         compiler_params=pltpu.CompilerParams(
             vmem_limit_bytes=60 * 1024 * 1024, collective_id=0, has_side_effects=True
         ),
     )(targets, points[0], cotangent[0], w_qkv, w_out, w_up, w_down)
-    wide = wide.astype(F32) * factor
-    last = last.astype(F32) * factor
-    return (
-        result[None],
-        grad_points[None],
-        last[:, 0 : 3 * C],
-        last[:, 3 * C :],
-        wide[:, 0:FF],
-        wide[:, FF:].T,
-    )
+    anywhere = pl.BlockSpec(memory_space=pl.ANY)
+    result, grad_points, *grads = pl.pallas_call(
+        lambda *refs: finish_kernel(factor, *refs),
+        out_shape=[
+            rows_type,
+            rows_type,
+            jax.ShapeDtypeStruct((C, 3 * C), F32),
+            jax.ShapeDtypeStruct((C, C), F32),
+            jax.ShapeDtypeStruct((C, FF), F32),
+            jax.ShapeDtypeStruct((FF, C), F32),
+        ],
+        in_specs=[anywhere] * 2 + [vmem] * 3,
+        out_specs=[anywhere] * 2 + [vmem] * 4,
+        scratch_shapes=[pltpu.SemaphoreType.DMA((2,))],
+    )(*gathered)
+    return (result[None], grad_points[None], *grads)
 
 
 def solution(mesh):

time: 167 us -> 198 us (1.19)
  Pallas kernels: 158 us -> 197 us
  local copies, waits for them, and re-layouts: 5.73 us -> 0 us
    pallas_call x0 -> x1, Pallas kernels: none -> 35.9 us  [body(): pl.pallas_call(lambda *refs: finish_kernel(factor, *refs), out_shape=[row...]
    pallas_call x1, Pallas kernels: 158 us -> 161 us  [body(): pl.pallas_call(lambda *refs: kernel(n_dp, list(names), *refs), out_shape=...]
    unnamed x9 -> x0, local copies, waits for them, and re-layouts: 2.9 us -> none
where the time goes in v3:
time: 198 us
  Pallas kernels  197 us (99%)
    pallas_call x1, Pallas kernels, body(): pl.pallas_call(lambda *refs: kernel(n_dp, list(names), *refs), out_shape=...  161 us
    pallas_call x1, Pallas kernels, body(): pl.pallas_call(lambda *refs: finish_kernel(factor, *refs), out_shape=[row...  35.9 us

profile of v3, /device:TPU:1, one launch (start us, length us, event | category | flops | bytes accessed | tf_op | source)
XLA Modules:
  0.0 198.2 jit_solution(7033141303723876587)
XLA Ops:
  0.6 161.5 %shard_map.118 = (bf16[1024,256]{1,0:T(8,128)(2,1)}, bf16[1024,256]{1,0:T(8,128)(2,1)}, bf16[256,2048]{1,0:T(8,128)(2,1)}, bf16[256,512]{1,0:T(8,128)(2,1)}, bf16[256,512]{1,0:T(8,128)(2,1)}) custom-call(s32[1,1024]{1,0:T(1,128)} %refs_0_.1, bf16[1024,256]{1,0:T(8,128)(2,1)} %bitcast.4, bf16[1024,256]{1,0:T(8,128)(2,1)} %bitcast.5, ...), custom_call_target="tpu_custom_call" | custom-call | tf_op jit(solution)/shard_map/pallas_call | solution.py:530
  162.1 35.9 %shard_map.119 = (bf16[1024,256]{1,0:T(8,128)(2,1)}, bf16[1024,256]{1,0:T(8,128)(2,1)}, f32[256,768]{1,0:T(8,128)}, f32[256,256]{1,0:T(8,128)}, f32[256,1024]{1,0:T(8,128)}, /*index=5*/f32[1024,256]{1,0:T(8,128)}) custom-call(bf16[1024,256]{1,0:T(8,128)(2,1)} %get-tuple-element.17.refs_0_, bf16[1024,256]{1,0:T(8,128)(2,1)} %get-tuple-element.18.refs_1_, ...), custom_call_target="tpu_custom_call" | custom-call | tf_op jit(solution)/shard_map/pallas_call | solution.py:547

commit v4 on v3

--- a/solution.py
+++ b/solution.py
@@ -247,29 +247,30 @@
 
 
 class Reduction:
-    def __init__(self, s, name, seq, zed, n_dp):
-        self.seq, self.zed, self.n_dp = seq, zed, n_dp
+    def __init__(self, s, name, outer, inner):
+        self.outer, self.inner = outer, inner
         self.own, self.got, self.cut, self.cut_got, self.fin, self.all = (
             getattr(s, name + part) for part in ("own", "got", "cut", "cutgot", "fin", "all")
         )
         sems = [(getattr(s, f"{name}send{i}"), getattr(s, f"{name}recv{i}")) for i in range(4)]
+        at, to = outer[2], inner[2]
         self.first = lambda: Copies(
-            "dp", n_dp, zed, 1, lambda d, p: self.own.at[p], lambda d: self.got.at[d], *sems[0]
+            *outer, 1, lambda d, p: self.own.at[p], lambda d: self.got.at[d], *sems[0]
         )
         self.second = lambda: Copies(
-            "seq", PEERS, seq, 1, lambda d, p: self.cut.at[p], lambda d: self.cut_got.at[d], *sems[1]
+            *inner, 1, lambda d, p: self.cut.at[p], lambda d: self.cut_got.at[d], *sems[1]
         )
         self.third = lambda: Copies(
-            "seq", PEERS, seq, 1, lambda d, p: self.fin.at[seq], lambda d: self.fin.at[seq], *sems[2]
+            *inner, 1, lambda d, p: self.fin.at[to], lambda d: self.fin.at[to], *sems[2]
         )
         self.fourth = lambda: Copies(
-            "dp", n_dp, zed, 1, lambda d, p: self.all.at[zed], lambda d: self.all.at[zed], *sems[3]
+            *outer, 1, lambda d, p: self.all.at[at], lambda d: self.all.at[at], *sems[3]
         )
 
     def spots(self):
         rows, cols = self.cut.shape[1:]
         across = self.own.shape[2] // cols
-        for piece in range(PEERS):
+        for piece in range(self.inner[1]):
             up, along = piece // across, piece % across
             yield piece, slice(up * rows, (up + 1) * rows), slice(along * cols, (along + 1) * cols)
 
@@ -279,18 +280,18 @@
     def step1(self):
         self.first().arrived()
         for piece, rows, cols in self.spots():
-            total = self.own[self.zed, rows, cols].astype(F32)
-            for d in range(1, self.n_dp):
+            total = self.own[self.outer[2], rows, cols].astype(F32)
+            for d in range(1, self.outer[1]):
                 total = total + self.got[d, rows, cols].astype(F32)
             self.cut[piece] = total
         self.second().start()
 
     def step2(self):
         self.second().arrived()
-        total = self.cut[self.seq]
-        for d in range(1, PEERS):
+        total = self.cut[self.inner[2]]
+        for d in range(1, self.inner[1]):
             total = total + self.cut_got[d]
-        self.fin[self.seq] = total
+        self.fin[self.inner[2]] = total
         self.third().start()
 
     def step3(self):
@@ -298,9 +299,9 @@
         across = self.own.shape[2] // self.cut.shape[2]
         bands = [
             jnp.concatenate([self.fin[at + piece] for piece in range(across)], axis=1)
-            for at in range(0, PEERS, across)
+            for at in range(0, self.inner[1], across)
         ]
-        self.all[self.zed] = jnp.concatenate(bands, axis=0).astype(BF)
+        self.all[self.outer[2]] = jnp.concatenate(bands, axis=0).astype(BF)
         self.fourth().start()
 
     def step4(self, out_ref):
@@ -335,15 +336,15 @@
     for name in ("place", "pts", "cot", "res", "grad"):
         names["send" + name] = sent((PEERS,))
         names["recv" + name] = sent((PEERS,))
-    for name, wide, piece in (
-        ("a", 2 * FF, (rows, HALF)),
-        ("b", 2 * C, (rows // 4, HALF)),
-        ("c", 2 * C, (rows // 4, HALF)),
+    for name, outer, inner, wide, piece in (
+        ("a", n_dp, PEERS, 2 * FF, (rows, HALF)),
+        ("b", n_dp, PEERS, 2 * C, (rows // 4, HALF)),
+        ("c", PEERS, n_dp, 2 * C, (C // PEERS // min(2, n_dp), 2 * C * min(2, n_dp) // n_dp)),
     ):
         for part in ("own", "got", "all"):
-            names[name + part] = pltpu.VMEM((n_dp, rows, wide), BF)
+            names[name + part] = pltpu.VMEM((outer, C // outer, wide), BF)
         for part in ("cut", "cutgot", "fin"):
-            names[name + part] = pltpu.VMEM((PEERS, *piece), F32)
+            names[name + part] = pltpu.VMEM((inner, *piece), F32)
         for step in range(4):
             names[f"{name}send{step}"] = sent((PEERS,))
             names[f"{name}recv{step}"] = sent((PEERS,))
@@ -395,7 +396,8 @@
                 piece = block[at * ROOM : (at + 1) * ROOM]
                 if d + at:
                     sent_ref[d + at] = piece
-                    go.start(d + at)
+                    if go is not None:
+                        go.start(d + at)
                 else:
                     own_ref[0] = piece
 
@@ -412,7 +414,7 @@
                 go_place.start(d + at)
             else:
                 s.place[0] = place
-    pack(cot, s.rcot, s.scot, go_cot)
+    pack(cot, s.rcot, s.scot, None)
 
     def send_back(go, rows_ref, mine_ref, theirs_ref):
         rows = rows_ref[...]
@@ -432,6 +434,7 @@
 
     go_place.arrived()
     go_pts.arrived()
+    go_cot.start()
     place_rows(s, s.rpts, s.x)
     first_part(s, w_qkv)
     attend(s)
@@ -443,11 +446,14 @@
     feed_forward(s, w_out, w_up, w_down)
     send_back(go_res, s.out, s.rres, s.sres)
 
-    wide, early, late = (Reduction(s, name, seq, zed, n_dp) for name in "abc")
+    along_seq, along_dp = ("seq", PEERS, seq), ("dp", n_dp, zed)
+    wide = Reduction(s, "a", along_dp, along_seq)
+    early = Reduction(s, "b", along_dp, along_seq)
+    late = Reduction(s, "c", along_seq, along_dp)
 
     def put(ref, values, at):
         ref[:, :, at : at + values.shape[1]] = values.astype(BF).reshape(
-            n_dp, C // n_dp, values.shape[1]
+            *ref.shape[0:2], values.shape[1]
         )
 
     put(s.aown, dot(transpose_bf(s.second[...]), s.gexp[...]), 0)
@@ -488,27 +494,24 @@
     normed, inverse = normalize(s.x[...].astype(F32))
     g_first = g_first.astype(BF).astype(F32)
     s.out[...] = (s.gh[...] + norm_back(normed, inverse, g_first)).astype(BF)
-    go_res.sent()
+    late.step1()
     send_back(go_grad, s.out, s.rgrad, s.sgrad)
-    late.step1()
+    late.step2()
     go_res.arrived()
     home_rows(s, s.rres, res_out)
-    late.step2()
+    late.step3()
     wide.step4(a_out)
-    late.step3()
     early.step4(b_out)
     go_grad.arrived()
     home_rows(s, s.rgrad, grad_out)
     late.step4(c_out)
-    for go in (go_place, go_pts, go_cot, go_grad):
+    for go in (go_place, go_pts, go_cot, go_res, go_grad):
         go.sent()
 
 
-def finish_kernel(factor, res, grad, a, b, c, res_out, grad_out, g_qkv, g_out, g_up, g_down, sems):
-    first = pltpu.make_async_copy(res, res_out, sems.at[0])
-    second = pltpu.make_async_copy(grad, grad_out, sems.at[1])
-    first.start()
-    second.start()
+def finish_kernel(factor, res, grad, a, b, c, res_out, grad_out, g_qkv, g_out, g_up, g_down):
+    res_out[...] = res[...]
+    grad_out[...] = grad[...]
     g_up[...] = a[:, 0:FF].astype(F32) * factor
     for at in range(0, FF, C):
         g_down[at : at + C, :] = a[:, FF + at : FF + at + C].astype(F32).T * factor
@@ -517,8 +520,6 @@
             at = part * C + half * HALF
             g_qkv[:, at : at + HALF] = ref[:, part * HALF : (part + 1) * HALF].astype(F32) * factor
         g_out[:, half * HALF : (half + 1) * HALF] = ref[:, 3 * HALF :].astype(F32) * factor
-    first.wait()
-    second.wait()
 
 
 def body(points, targets, cotangent, w_qkv, w_out, w_up, w_down):
@@ -543,7 +544,6 @@
             vmem_limit_bytes=60 * 1024 * 1024, collective_id=0, has_side_effects=True
         ),
     )(targets, points[0], cotangent[0], w_qkv, w_out, w_up, w_down)
-    anywhere = pl.BlockSpec(memory_space=pl.ANY)
     result, grad_points, *grads = pl.pallas_call(
         lambda *refs: finish_kernel(factor, *refs),
         out_shape=[
@@ -554,9 +554,8 @@
             jax.ShapeDtypeStruct((C, FF), F32),
             jax.ShapeDtypeStruct((FF, C), F32),
         ],
-        in_specs=[anywhere] * 2 + [vmem] * 3,
-        out_specs=[anywhere] * 2 + [vmem] * 4,
-        scratch_shapes=[pltpu.SemaphoreType.DMA((2,))],
+        in_specs=[vmem] * 5,
+        out_specs=[vmem] * 6,
     )(*gathered)
     return (result[None], grad_points[None], *grads)
 

time: 198 us -> 154 us (0.78)
  Pallas kernels: 197 us -> 152 us
    pallas_call x1, Pallas kernels: 35.9 us -> 3.85 us  [body(): pl.pallas_call(lambda *refs: finish_kernel(factor, *refs), out_shape=[row...]
    pallas_call x1, Pallas kernels: 161 us -> 149 us  [body(): pl.pallas_call(lambda *refs: kernel(n_dp, list(names), *refs), out_shape=...]
where the time goes in v4:
time: 154 us; the launch traced here: 153 us
  Pallas kernels  152 us (99%)
    pallas_call x1, Pallas kernels, body(): pl.pallas_call(lambda *refs: kernel(n_dp, list(names), *refs), out_shape=...  149 us
    pallas_call x1, Pallas kernels, body(): pl.pallas_call(lambda *refs: finish_kernel(factor, *refs), out_shape=[row...  3.85 us

profile of v4, /device:TPU:1, one launch (start us, length us, event | category | flops | bytes accessed | tf_op | source)
XLA Modules:
  0.0 153.0 jit_solution(11790907484761178854)
XLA Ops:
  0.6 148.5 %shard_map.118 = (bf16[1024,256]{1,0:T(8,128)(2,1)}, bf16[1024,256]{1,0:T(8,128)(2,1)}, bf16[256,2048]{1,0:T(8,128)(2,1)}, bf16[256,512]{1,0:T(8,128)(2,1)}, bf16[256,512]{1,0:T(8,128)(2,1)}) custom-call(s32[1,1024]{1,0:T(1,128)} %refs_0_.1, bf16[1024,256]{1,0:T(8,128)(2,1)} %bitcast.4, bf16[1024,256]{1,0:T(8,128)(2,1)} %bitcast.5, ...), custom_call_target="tpu_custom_call" | custom-call | tf_op jit(solution)/shard_map/pallas_call | solution.py:531
  149.2 3.9 %shard_map.119 = (bf16[1024,256]{1,0:T(8,128)(2,1)}, bf16[1024,256]{1,0:T(8,128)(2,1)}, f32[256,768]{1,0:T(8,128)}, f32[256,256]{1,0:T(8,128)}, f32[256,1024]{1,0:T(8,128)}, /*index=5*/f32[1024,256]{1,0:T(8,128)}) custom-call(bf16[1024,256]{1,0:T(8,128)(2,1)} %get-tuple-element.17.refs_0_, bf16[1024,256]{1,0:T(8,128)(2,1)} %get-tuple-element.18.refs_1_, ...), custom_call_target="tpu_custom_call" | custom-call | tf_op jit(solution)/shard_map/pallas_call | solution.py:547

commit v5 on v4

--- a/solution.py
+++ b/solution.py
@@ -308,6 +308,49 @@
         self.fourth().arrived()
         out_ref[...] = self.all[...].reshape(out_ref.shape)
         for copies in (self.first, self.second, self.third, self.fourth):
+            copies().sent()
+
+
+class ShortReduction:
+    def __init__(self, s, name, seq, zed, n_dp):
+        self.seq, self.zed, self.n_dp = seq, zed, n_dp
+        self.own, self.got, self.mid, self.all = (
+            getattr(s, name + part) for part in ("own", "got", "mid", "all")
+        )
+        sems = [(getattr(s, f"{name}send{i}"), getattr(s, f"{name}recv{i}")) for i in range(3)]
+        self.first = lambda: Copies(
+            "seq", PEERS, seq, 1, lambda d, p: self.own.at[p], lambda d: self.got.at[d], *sems[0]
+        )
+        self.second = lambda: Copies(
+            "dp", n_dp, zed, 1, lambda d, p: self.mid.at[zed], lambda d: self.mid.at[zed], *sems[1]
+        )
+        self.third = lambda: Copies(
+            "seq", PEERS, seq, 1, lambda d, p: self.all.at[seq], lambda d: self.all.at[seq], *sems[2]
+        )
+
+    def step0(self):
+        self.first().start()
+
+    def step1(self):
+        self.first().arrived()
+        total = self.own[self.seq].astype(F32)
+        for d in range(1, PEERS):
+            total = total + self.got[d].astype(F32)
+        self.mid[self.zed] = total.astype(BF)
+        self.second().start()
+
+    def step2(self):
+        self.second().arrived()
+        total = self.mid[0].astype(F32)
+        for other in range(1, self.n_dp):
+            total = total + self.mid[other].astype(F32)
+        self.all[self.seq] = total.astype(BF)
+        self.third().start()
+
+    def step3(self, out_ref):
+        self.third().arrived()
+        out_ref[...] = self.all[...].reshape(out_ref.shape)
+        for copies in (self.first, self.second, self.third):
             copies().sent()
 
 
@@ -339,7 +382,6 @@
     for name, outer, inner, wide, piece in (
         ("a", n_dp, PEERS, 2 * FF, (rows, HALF)),
         ("b", n_dp, PEERS, 2 * C, (rows // 4, HALF)),
-        ("c", PEERS, n_dp, 2 * C, (C // PEERS // min(2, n_dp), 2 * C * min(2, n_dp) // n_dp)),
     ):
         for part in ("own", "got", "all"):
             names[name + part] = pltpu.VMEM((outer, C // outer, wide), BF)
@@ -348,6 +390,12 @@
         for step in range(4):
             names[f"{name}send{step}"] = sent((PEERS,))
             names[f"{name}recv{step}"] = sent((PEERS,))
+    for part in ("own", "got", "all"):
+        names["c" + part] = pltpu.VMEM((PEERS, C // PEERS, 2 * C), BF)
+    names["cmid"] = pltpu.VMEM((n_dp, C // PEERS, 2 * C), BF)
+    for step in range(3):
+        names[f"csend{step}"] = sent((PEERS,))
+        names[f"crecv{step}"] = sent((PEERS,))
     return names
 
 
@@ -449,7 +497,7 @@
     along_seq, along_dp = ("seq", PEERS, seq), ("dp", n_dp, zed)
     wide = Reduction(s, "a", along_dp, along_seq)
     early = Reduction(s, "b", along_dp, along_seq)
-    late = Reduction(s, "c", along_seq, along_dp)
+    late = ShortReduction(s, "c", seq, zed, n_dp)
 
     def put(ref, values, at):
         ref[:, :, at : at + values.shape[1]] = values.astype(BF).reshape(
@@ -494,17 +542,16 @@
     normed, inverse = normalize(s.x[...].astype(F32))
     g_first = g_first.astype(BF).astype(F32)
     s.out[...] = (s.gh[...] + norm_back(normed, inverse, g_first)).astype(BF)
+    send_back(go_grad, s.out, s.rgrad, s.sgrad)
     late.step1()
-    send_back(go_grad, s.out, s.rgrad, s.sgrad)
-    late.step2()
     go_res.arrived()
     home_rows(s, s.rres, res_out)
-    late.step3()
+    late.step2()
     wide.step4(a_out)
     early.step4(b_out)
     go_grad.arrived()
     home_rows(s, s.rgrad, grad_out)
-    late.step4(c_out)
+    late.step3(c_out)
     for go in (go_place, go_pts, go_cot, go_res, go_grad):
         go.sent()
 

time: 154 us -> 154 us (level)
  no operation moved by 1% of the time
where the time goes in v5:
time: 154 us
  Pallas kernels  153 us (99%)
    pallas_call x1, Pallas kernels, body(): pl.pallas_call(lambda *refs: kernel(n_dp, list(names), *refs), out_shape=...  150 us
    pallas_call x1, Pallas kernels, body(): pl.pallas_call(lambda *refs: finish_kernel(factor, *refs), out_shape=[row...  3.85 us

profile of v5, /device:TPU:1, one launch (start us, length us, event | category | flops | bytes accessed | tf_op | source)
XLA Modules:
  0.0 154.1 jit_solution(15932378795910331321)
XLA Ops:
  0.6 149.6 %shard_map.118 = (bf16[1024,256]{1,0:T(8,128)(2,1)}, bf16[1024,256]{1,0:T(8,128)(2,1)}, bf16[256,2048]{1,0:T(8,128)(2,1)}, bf16[256,512]{1,0:T(8,128)(2,1)}, bf16[256,512]{1,0:T(8,128)(2,1)}) custom-call(s32[1,1024]{1,0:T(1,128)} %refs_0_.1, bf16[1024,256]{1,0:T(8,128)(2,1)} %bitcast.4, bf16[1024,256]{1,0:T(8,128)(2,1)} %bitcast.5, ...), custom_call_target="tpu_custom_call" | custom-call | tf_op jit(solution)/shard_map/pallas_call | solution.py:578
  150.2 3.9 %shard_map.119 = (bf16[1024,256]{1,0:T(8,128)(2,1)}, bf16[1024,256]{1,0:T(8,128)(2,1)}, f32[256,768]{1,0:T(8,128)}, f32[256,256]{1,0:T(8,128)}, f32[256,1024]{1,0:T(8,128)}, /*index=5*/f32[1024,256]{1,0:T(8,128)}) custom-call(bf16[1024,256]{1,0:T(8,128)(2,1)} %get-tuple-element.17.refs_0_, bf16[1024,256]{1,0:T(8,128)(2,1)} %get-tuple-element.18.refs_1_, ...), custom_call_target="tpu_custom_call" | custom-call | tf_op jit(solution)/shard_map/pallas_call | solution.py:594

commit v6 on v4

--- a/solution.py
+++ b/solution.py
@@ -348,6 +348,10 @@
         for step in range(4):
             names[f"{name}send{step}"] = sent((PEERS,))
             names[f"{name}recv{step}"] = sent((PEERS,))
+    shapes = ((1, ROWS), tall, tall, (C, 3 * C), (C, C), (C, FF), (FF, C))
+    for at, shape in enumerate(shapes):
+        names[f"in{at}"] = pltpu.VMEM(shape, BF if at else jnp.int32)
+    names["loaded"] = sent((7,))
     return names
 
 
@@ -358,11 +362,25 @@
 
 
 def kernel(
-    n_dp, names, tgt, pts, cot, w_qkv, w_out, w_up, w_down,
+    n_dp, names, tgt_in, pts_in, cot_in, qkv_in, out_in, up_in, down_in,
     res_out, grad_out, a_out, b_out, c_out, *refs,
 ):
     s = Scratch(names, refs)
     seq, zed = lax.axis_index("seq"), lax.axis_index("dp")
+    tgt, pts, cot, w_qkv, w_out, w_up, w_down = (
+        getattr(s, f"in{at}") for at in range(7)
+    )
+    loads = [
+        pltpu.make_async_copy(source, target, s.loaded.at[at])
+        for at, (source, target) in enumerate(
+            (
+                (tgt_in, tgt), (pts_in, pts), (cot_in, cot), (qkv_in, w_qkv),
+                (out_in, w_out), (up_in, w_up), (down_in, w_down),
+            )
+        )
+    ]
+    for load in loads:
+        load.start()
     barrier = pltpu.get_barrier_semaphore()
     for axis, size, me in (("seq", PEERS, seq), ("dp", n_dp, zed)):
         for d in range(1, size):
@@ -385,6 +403,7 @@
     go_res = exchange("res", -1, s.sres, s.rres)
     go_grad = exchange("grad", -1, s.sgrad, s.rgrad)
 
+    loads[0].wait()
     slot, aux = slot_rows(tgt[...], seq)
     s.slot[...] = slot
     pl.semaphore_wait(barrier, PEERS - 1 + n_dp - 1)
@@ -401,6 +420,7 @@
                 else:
                     own_ref[0] = piece
 
+    loads[1].wait()
     pack(pts, s.rpts, s.spts, go_pts)
     for d in (4, 8, 12, 0):
         found = dot_nt(aux, one_hot(iota((4 * ROOM, ROWS), 0) + d * ROOM == slot))
@@ -414,6 +434,8 @@
                 go_place.start(d + at)
             else:
                 s.place[0] = place
+    for load in loads[2:]:
+        load.wait()
     pack(cot, s.rcot, s.scot, None)
 
     def send_back(go, rows_ref, mine_ref, theirs_ref):
@@ -474,19 +496,13 @@
     def half_way():
         put_heads(s.bown, 0)
         early.step0()
-        wide.step3()
+        wide.step2()
 
     attend_back(
         s,
-        {
-            2: wide.step1,
-            3: wide.step2,
-            4: half_way,
-            5: early.step1,
-            6: early.step2,
-            7: early.step3,
-        },
+        {3: wide.step1, 4: half_way, 5: wide.step3, 6: early.step1, 7: early.step2},
     )
+    early.step3()
     put_heads(s.cown, 1)
     late.step0()
     g_first = dot_nt(s.dq[...], w_qkv[:, 0:C]) + dot_nt(s.dk[...].astype(BF), w_qkv[:, C : 2 * C])
@@ -494,8 +510,8 @@
     normed, inverse = normalize(s.x[...].astype(F32))
     g_first = g_first.astype(BF).astype(F32)
     s.out[...] = (s.gh[...] + norm_back(normed, inverse, g_first)).astype(BF)
+    send_back(go_grad, s.out, s.rgrad, s.sgrad)
     late.step1()
-    send_back(go_grad, s.out, s.rgrad, s.sgrad)
     late.step2()
     go_res.arrived()
     home_rows(s, s.rres, res_out)
@@ -537,11 +553,11 @@
             jax.ShapeDtypeStruct((C, 2 * C), BF),
             jax.ShapeDtypeStruct((C, 2 * C), BF),
         ],
-        in_specs=[vmem] * 7,
+        in_specs=[pl.BlockSpec(memory_space=pltpu.HBM)] * 7,
         out_specs=[vmem] * 5,
         scratch_shapes=list(names.values()),
         compiler_params=pltpu.CompilerParams(
-            vmem_limit_bytes=60 * 1024 * 1024, collective_id=0, has_side_effects=True
+            vmem_limit_bytes=61 * 1024 * 1024, collective_id=0, has_side_effects=True
         ),
     )(targets, points[0], cotangent[0], w_qkv, w_out, w_up, w_down)
     result, grad_points, *grads = pl.pallas_call(

time: 154 us -> 154 us (level)
  no operation moved by 1% of the time
where the time goes in v6:
time: 154 us
  Pallas kernels  153 us (99%)
    pallas_call x1, Pallas kernels, body(): pl.pallas_call(lambda *refs: kernel(n_dp, list(names), *refs), out_shape=...  149 us
    pallas_call x1, Pallas kernels, body(): pl.pallas_call(lambda *refs: finish_kernel(factor, *refs), out_shape=[row...  3.85 us

profile of v6, /device:TPU:1, one launch (start us, length us, event | category | flops | bytes accessed | tf_op | source)
XLA Modules:
  0.0 154.0 jit_solution(1373634545341261920)
XLA Ops:
  0.6 149.5 %shard_map.118 = (bf16[1024,256]{1,0:T(8,128)(2,1)}, bf16[1024,256]{1,0:T(8,128)(2,1)}, bf16[256,2048]{1,0:T(8,128)(2,1)}, bf16[256,512]{1,0:T(8,128)(2,1)}, bf16[256,512]{1,0:T(8,128)(2,1)}) custom-call(s32[1,1024]{1,0:T(1,128)} %refs_0_.1, bf16[1024,256]{1,0:T(8,128)(2,1)} %bitcast.4, bf16[1024,256]{1,0:T(8,128)(2,1)} %bitcast.5, ...), custom_call_target="tpu_custom_call" | custom-call | tf_op jit(solution)/shard_map/pallas_call | solution.py:547
  150.1 3.9 %shard_map.119 = (bf16[1024,256]{1,0:T(8,128)(2,1)}, bf16[1024,256]{1,0:T(8,128)(2,1)}, f32[256,768]{1,0:T(8,128)}, f32[256,256]{1,0:T(8,128)}, f32[256,1024]{1,0:T(8,128)}, /*index=5*/f32[1024,256]{1,0:T(8,128)}) custom-call(bf16[1024,256]{1,0:T(8,128)(2,1)} %get-tuple-element.17.refs_0_, bf16[1024,256]{1,0:T(8,128)(2,1)} %get-tuple-element.18.refs_1_, ...), custom_call_target="tpu_custom_call" | custom-call | tf_op jit(solution)/shard_map/pallas_call | solution.py:563

commit v7 on v5

--- a/solution.py
+++ b/solution.py
@@ -542,8 +542,8 @@
     normed, inverse = normalize(s.x[...].astype(F32))
     g_first = g_first.astype(BF).astype(F32)
     s.out[...] = (s.gh[...] + norm_back(normed, inverse, g_first)).astype(BF)
+    late.step1()
     send_back(go_grad, s.out, s.rgrad, s.sgrad)
-    late.step1()
     go_res.arrived()
     home_rows(s, s.rres, res_out)
     late.step2()

time: 154 us -> 154 us (level)
  no operation moved by 1% of the time
where the time goes in v7:
time: 154 us; the launch traced here: 153 us
  Pallas kernels  152 us (99%)
    pallas_call x1, Pallas kernels, body(): pl.pallas_call(lambda *refs: kernel(n_dp, list(names), *refs), out_shape=...  148 us
    pallas_call x1, Pallas kernels, body(): pl.pallas_call(lambda *refs: finish_kernel(factor, *refs), out_shape=[row...  3.85 us

profile of v7, /device:TPU:1, one launch (start us, length us, event | category | flops | bytes accessed | tf_op | source)
XLA Modules:
  0.0 152.7 jit_solution(3962291083097965598)
XLA Ops:
  0.6 148.2 %shard_map.118 = (bf16[1024,256]{1,0:T(8,128)(2,1)}, bf16[1024,256]{1,0:T(8,128)(2,1)}, bf16[256,2048]{1,0:T(8,128)(2,1)}, bf16[256,512]{1,0:T(8,128)(2,1)}, bf16[256,512]{1,0:T(8,128)(2,1)}) custom-call(s32[1,1024]{1,0:T(1,128)} %refs_0_.1, bf16[1024,256]{1,0:T(8,128)(2,1)} %bitcast.4, bf16[1024,256]{1,0:T(8,128)(2,1)} %bitcast.5, ...), custom_call_target="tpu_custom_call" | custom-call | tf_op jit(solution)/shard_map/pallas_call | solution.py:578
  148.9 3.9 %shard_map.119 = (bf16[1024,256]{1,0:T(8,128)(2,1)}, bf16[1024,256]{1,0:T(8,128)(2,1)}, f32[256,768]{1,0:T(8,128)}, f32[256,256]{1,0:T(8,128)}, f32[256,1024]{1,0:T(8,128)}, /*index=5*/f32[1024,256]{1,0:T(8,128)}) custom-call(bf16[1024,256]{1,0:T(8,128)(2,1)} %get-tuple-element.17.refs_0_, bf16[1024,256]{1,0:T(8,128)(2,1)} %get-tuple-element.18.refs_1_, ...), custom_call_target="tpu_custom_call" | custom-call | tf_op jit(solution)/shard_map/pallas_call | solution.py:594
